TPU v7x, 32 devices: a whole 2x2x4 slice. The times are simulated.
32 devices in a mesh: mem: 2 (over x), gy: 4 (over z), gx: 4 (over y, core).
Axes of the slice: x: 2, y: 2, z: 4, core: 2. Of those that a mesh axis runs over, the one named last changes fastest.
Arguments:
- alpha: float32 [16, 32, 64, 512], P('mem', None, 'gy', 'gx'), may hold values from -4 to 4
- perturb: bfloat16 [16, 4, 32, 64, 512], P('mem', None, None, 'gy', 'gx'), may hold values from -6 to 6
- chi: float32 [4, 32, 64, 512], P(None, None, 'gy', 'gx'), may hold values from -4 to 4
- kappa: float32 [64, 512], P('gy', 'gx'), may hold values from 0.05 to 0.24
- vert_bounds: int32 [2, 32], replicated, may hold values from 0 to 31, as said below
- static_vert: float32 [4, 32, 32], replicated, may hold values from -1 to 1
- fine_owner: int32 [16, 2], P(('gy', 'gx')), may hold values from 0 to 1, each once within a row
- obs_stencil: int32 [32768], P(('mem', 'gy', 'gx')), may hold values from 0 to 959
- obs_weight: float32 [4, 32768], P(None, ('mem', 'gy', 'gx')), may hold values from 0.05 to 0.5
- background: bfloat16 [32768, 128], P(('mem', 'gy', 'gx')), may hold values from -6 to 6
- observed: float32 [8, 32768], P(None, ('mem', 'gy', 'gx')), may hold values from -6 to 6
- inv_var: float32 [8, 32768], P(None, ('mem', 'gy', 'gx')), may hold values from 2 to 32
- jacobian: float32 [8, 128], replicated, may hold values from -0.5 to 0.5
- obs_count: int32 [32], P(('mem', 'gy', 'gx')), may hold values from 256 to 1024, as said below
Outputs:
- grad_alpha: float32 [16, 32, 64, 512], P('mem', None, 'gy', 'gx')
- grad_chi: float32 [4, 32, 64, 512], P(None, None, 'gy', 'gx')
Inputs may be any that keep to these rules, and one draw needn't show every extreme that they name: `vert_bounds`: row 0 holds each level's lowest and row 1 its highest coupled level; level l lies between both inclusive, and each lies 1 to 4 levels from l unless cut at the ends of the column. `obs_count`: observations below this count in a device's block are live; some device has exactly 1024 and some exactly 256.
All inputs are finite; a program needn't handle non-finite values.
Results may differ from a plain program's by a relative error of at most 0.00099.
Values may be sent and summed in bfloat16 or wider, within the bound.
A program may use at most 128 MiB of HBM per device.

v0:
```python
import math

import jax
import jax.numpy as jnp
from jax import lax
from jax.experimental import pallas as pl
from jax.experimental.pallas import tpu as pltpu
from jax.sharding import PartitionSpec as P

NDIFF = 4

ensemble_weight = 0.8
static_weight = 0.6
vertical_scale = 2.0
highest = lax.Precision.HIGHEST
f32 = jnp.float32
bf16 = jnp.bfloat16
NT = (((1,), (1,)), ((), ()))
TN = (((0,), (0,)), ((), ()))


def shifted(value, axis, steps):
    count = lax.axis_size(axis)
    pairs = [(source, (source + steps) % count) for source in range(count)]
    return lax.ppermute(value, axis, pairs)


def params(grid_dims=0):
    if grid_dims:
        return pltpu.CompilerParams(
            dimension_semantics=("arbitrary",) * grid_dims, vmem_limit_bytes=56 << 20
        )
    return pltpu.CompilerParams(vmem_limit_bytes=56 << 20)


SIDE = 8
NN = (((1,), (0,)), ((), ()))


def compass():
    gx, gy = lax.axis_index("gx"), lax.axis_index("gy")
    gx_count, gy_count = lax.axis_size("gx"), lax.axis_size("gy")
    east, west = lax.rem(gx + 1, gx_count), lax.rem(gx + gx_count - 1, gx_count)
    return east, west, gy - 1, gy + 1, gy > 0, gy < gy_count - 1


def greet_around():
    east, west, north, south, has_north, has_south = compass()
    barrier = pltpu.get_barrier_semaphore()

    def greet(device):
        pl.semaphore_signal(
            barrier, inc=1, device_id=device, device_id_type=pl.DeviceIdType.MESH
        )

    greet({"gx": east})
    greet({"gx": west})

    @pl.when(has_north)
    def _():
        for device in ({"gy": north}, {"gy": north, "gx": east}, {"gy": north, "gx": west}):
            greet(device)

    @pl.when(has_south)
    def _():
        for device in ({"gy": south}, {"gy": south, "gx": east}, {"gy": south, "gx": west}):
            greet(device)


def wait_around():
    east, west, north, south, has_north, has_south = compass()
    peers = 2 + 3 * has_north.astype(jnp.int32) + 3 * has_south.astype(jnp.int32)
    pl.semaphore_wait(pltpu.get_barrier_semaphore(), peers)


def ring_copies(dims, ring, first_rows, last_rows, south_in, north_in, send, recv):
    rows, levels, width, variables, depth = dims
    east, west, north, south, has_north, has_south = compass()
    top, bottom = pl.ds(depth, depth), pl.ds(rows, depth)
    body, above, below = pl.ds(depth, rows), pl.ds(0, depth), pl.ds(depth + rows, depth)
    first, last = pl.ds(2 * SIDE, SIDE), pl.ds(SIDE + width, SIDE)
    before, after = pl.ds(SIDE, SIDE), pl.ds(2 * SIDE + width, SIDE)

    def copy(source, target, place, device):
        return pltpu.make_async_remote_copy(
            src_ref=source, dst_ref=target, send_sem=send.at[place], recv_sem=recv.at[place],
            device_id=device, device_id_type=pl.DeviceIdType.MESH,
        )

    across = [
        copy(ring.at[body, last], ring.at[body, before], 0, {"gx": east}),
        copy(ring.at[body, first], ring.at[body, after], 1, {"gx": west}),
    ]
    up = [
        copy(first_rows, south_in, 2, {"gy": north}),
        copy(ring.at[top, last], ring.at[below, before], 3, {"gy": north, "gx": east}),
        copy(ring.at[top, first], ring.at[below, after], 4, {"gy": north, "gx": west}),
    ]
    down = [
        copy(last_rows, north_in, 5, {"gy": south}),
        copy(ring.at[bottom, last], ring.at[above, before], 6, {"gy": south, "gx": east}),
        copy(ring.at[bottom, first], ring.at[above, after], 7, {"gy": south, "gx": west}),
    ]

    def start():
        @pl.when(has_north)
        def _():
            for item in up:
                item.start()

        @pl.when(has_south)
        def _():
            for item in down:
                item.start()

        for item in across:
            item.start()

    def wait():
        for item in across:
            item.wait_recv()
            item.wait_send()

        @pl.when(has_north)
        def _():
            for item in down:
                item.wait_recv()
            for item in up:
                item.wait_send()

        @pl.when(has_south)
        def _():
            for item in up:
                item.wait_recv()
            for item in down:
                item.wait_send()

    return start, wait


def fill_halo_rows(dims, ring, from_south, from_north):
    rows, levels, width, variables, depth = dims
    east, west, north, south, has_north, has_south = compass()
    inner, whole = pl.ds(2 * SIDE, width), pl.ds(SIDE, width + 2 * SIDE)

    @pl.when(has_south)
    def _():
        for d in range(depth):
            ring[depth + rows + d, inner] = from_south(d)

    @pl.when(jnp.logical_not(has_south))
    def _():
        for d in range(depth):
            ring[depth + rows + d, whole] = ring[depth + rows - 1 - d, whole]

    @pl.when(has_north)
    def _():
        for d in range(depth):
            ring[d, inner] = from_north(d)

    @pl.when(jnp.logical_not(has_north))
    def _():
        for d in range(depth):
            ring[d, whole] = ring[2 * depth - 1 - d, whole]


def diffuse(dims, ring, work, kap):
    rows, levels, width, variables, depth = dims
    for step in range(1, depth + 1):
        source, target = (ring, work) if step % 2 else (work, ring)
        start, stop = (SIDE, width + 3 * SIDE) if step < depth else (2 * SIDE, width + 2 * SIDE)

        @pl.loop(0, rows // 2 + depth - step)
        def _(pair, source=source, target=target, start=start, stop=stop, step=step):
            y = step + 2 * pair
            for x in range(start, stop, 6 * SIDE):
                size = min(6 * SIDE, stop - x)
                here = pl.ds(x, size)
                held = [source[y + i, here] for i in (-1, 0, 1, 2)]
                for i in (0, 1):
                    center = held[i + 1]
                    sides = source[y + i, pl.ds(x - 1, size)] + source[y + i, pl.ds(x + 1, size)]
                    change = (held[i] + held[i + 2]) + sides - 4.0 * center
                    target[y + i, here] = center + kap[y + i, here] * change


def split(value):
    high = value.astype(bf16)
    return high, (value - high.astype(f32)).astype(bf16)


def stacked_weights(weights):
    high, low = split(weights)
    return jnp.concatenate(
        [
            jnp.concatenate([high, high], axis=1),
            jnp.concatenate([low, jnp.zeros_like(low)], axis=1),
        ],
        axis=0,
    )


def mixed(weights_ref, value, axis):
    half = weights_ref.shape[0] // 2
    numbers = NT if axis else NN
    both = lax.dot_general(
        weights_ref[...], jnp.concatenate(split(value), axis=axis), numbers,
        preferred_element_type=f32,
    )
    return both[:half] + both[half:]


def lane_grid(lanes, levels):
    row = lax.broadcasted_iota(jnp.int32, (lanes, lanes), 0)
    col = lax.broadcasted_iota(jnp.int32, (lanes, lanes), 1)
    row_block, col_block = row // levels, col // levels
    return row - row_block * levels, col - col_block * levels, row_block == col_block


def vertical_blocks(bounds_ref, lanes, levels, transposed):
    row, col, same = lane_grid(lanes, levels)
    bounds = bounds_ref[...].astype(f32)
    limits = []
    for side in range(2):
        line = jnp.concatenate([bounds[side : side + 1]] * (lanes // levels), axis=1)
        spread = jnp.broadcast_to(line, (lanes, lanes))
        limits.append(spread if transposed else spread.T)
    reach = (row if transposed else col).astype(f32)
    distance = jnp.abs(row - col).astype(f32)
    inside = same & (reach >= limits[0]) & (reach <= limits[1])
    return jnp.where(inside, jnp.exp(-distance / vertical_scale), 0.0)


def static_blocks(static_ref, levels):
    variables = static_ref.shape[0]
    lanes = variables * levels
    same = lane_grid(lanes, levels)[2]
    tiles = [jnp.concatenate([static_ref[v]] * variables, axis=1) for v in range(variables)]
    return jnp.where(same, jnp.concatenate(tiles, axis=0), 0.0)


def pack_row(dims, ring, first_rows, last_rows, y, value):
    rows, levels, width, variables, depth = dims
    ring[depth + y, pl.ds(2 * SIDE, width)] = value
    if y < depth:
        first_rows[y] = value.astype(bf16)
    if y >= rows - depth:
        last_rows[y - (rows - depth)] = value.astype(bf16)


def forward_kernel(
    dims, ens_scale, bounds, static_vert, kappa, alpha_hbm, chi_hbm, perturb_hbm, out, kap,
    alpha, chi, perturb, ring, work, rows_out, rows_in, kappa_in, spread, acc, static, mix, load,
    send, recv,
):
    rows, levels, width, variables, depth = dims
    groups, lanes = ring.shape[0], ring.shape[3]
    count, column = rows * levels, variables * levels
    group_rows = lanes * rows
    greet_around()
    loads = [
        pltpu.make_async_copy(
            alpha_hbm.at[pl.ds(g * group_rows, group_rows)],
            alpha.at[pl.ds(g * group_rows, group_rows)], load.at[g],
        )
        for g in range(groups)
    ]
    load_chi = pltpu.make_async_copy(chi_hbm, chi, load.at[groups])
    load_perturb = pltpu.make_async_copy(perturb_hbm, perturb, load.at[groups + 1])
    for item in loads:
        item.start()
    load_chi.start()
    load_perturb.start()
    for y in range(rows):
        kap[depth + y, pl.ds(2 * SIDE, width)] = jnp.broadcast_to(
            kappa[y : y + 1, :], (lanes, width)
        ).T
    moves = [
        ring_copies(
            dims, ring.at[g], rows_out.at[g, 0], rows_out.at[g, 1], rows_in.at[g, 0],
            rows_in.at[g, 1], send.at[g], recv.at[g],
        )
        for g in range(groups)
    ]
    move_kappa = ring_copies(
        dims, kap, kappa.at[pl.ds(0, SIDE)], kappa.at[pl.ds(rows - SIDE, SIDE)], kappa_in.at[0],
        kappa_in.at[1], send.at[groups], recv.at[groups],
    )
    for g in range(groups):
        loads[g].wait()
        for y in range(rows):
            block = alpha[pl.ds(g * group_rows + y, lanes, stride=rows), :]
            pack_row(dims, ring.at[g], rows_out.at[g, 0], rows_out.at[g, 1], y, block.T)
        if g == 0:
            wait_around()
        moves[g][0]()
        if g == 0:
            move_kappa[0]()
    mix[...] = stacked_weights(
        static_blocks(static_vert, levels)
        * jnp.where(lax.axis_index("mem") == 0, static_weight, 0.0)
    )
    load_chi.wait()
    for y in range(rows):
        static[y] = mixed(mix, chi[pl.ds(y, column, stride=rows), :], 0)
    mix[...] = stacked_weights(vertical_blocks(bounds, lanes, levels, False))
    move_kappa[1]()
    fill_halo_rows(
        dims, kap,
        lambda d: jnp.broadcast_to(kappa_in[0, d : d + 1, :], (lanes, width)).T,
        lambda d: jnp.broadcast_to(
            kappa_in[1, SIDE - depth + d : SIDE - depth + d + 1, :], (lanes, width)
        ).T,
    )
    for g in range(groups):
        moves[g][1]()
        fill_halo_rows(
            dims, ring.at[g], lambda d: rows_in[g, 0, d].astype(f32),
            lambda d: rows_in[g, 1, d].astype(f32),
        )
        diffuse(dims, ring.at[g], work, kap)
        for y in range(rows):
            spread[pl.ds(g * group_rows + y, lanes, stride=rows), :] = mixed(
                mix, ring[g, depth + y, pl.ds(2 * SIDE, width)], 1
            )
    load_perturb.wait()
    members = perturb.shape[0]

    @pl.loop(0, levels)
    def _(level):
        place = pl.multiple_of(level * rows, rows)
        spreads = [spread[pl.ds(k * count + place, rows), :] for k in range(members)]
        for v in range(variables):
            total = perturb[0, v, pl.ds(place, rows), :].astype(f32) * spreads[0]
            for k in range(1, members):
                total = total + perturb[k, v, pl.ds(place, rows), :].astype(f32) * spreads[k]
            acc[pl.ds(v * count + place, rows), :] = total

    for y in range(rows):
        out[y] = (ens_scale * acc[pl.ds(y, column, stride=rows), :] + static[y]).T


def backward_kernel(
    dims, ens_scale, bounds, static_vert, kappa, grad, kap, alpha_hbm, chi_hbm, perturb_hbm,
    out_alpha, out_chi, alpha, chi, perturb, ring, work, rows_out, rows_in, field, nat, mix, load,
    send, recv,
):
    rows, levels, width, variables, depth = dims
    groups, lanes = ring.shape[0], ring.shape[3]
    count, column = rows * levels, variables * levels
    group_rows = lanes * rows
    group_members = lanes // levels
    inner = pl.ds(2 * SIDE, width)
    greet_around()
    loads = [
        pltpu.make_async_copy(
            perturb_hbm.at[pl.ds(g * group_members, group_members)],
            perturb.at[pl.ds(g * group_members, group_members)], load.at[g],
        )
        for g in range(groups)
    ]
    load_chi = pltpu.make_async_copy(chi_hbm, chi, load.at[groups])
    load_alpha = pltpu.make_async_copy(alpha_hbm, alpha, load.at[groups + 1])
    for item in loads:
        item.start()
    load_chi.start()
    load_alpha.start()
    for y in range(rows):
        nat[pl.ds(y, column, stride=rows), :] = ens_scale * grad[y].T
    moves = [
        ring_copies(
            dims, ring.at[g], rows_out.at[g, 0], rows_out.at[g, 1], rows_in.at[g, 0],
            rows_in.at[g, 1], send.at[g], recv.at[g],
        )
        for g in range(groups)
    ]
    for g in range(groups):
        loads[g].wait()

        @pl.loop(0, levels)
        def _(level, g=g):
            place = pl.multiple_of(level * rows, rows)
            slopes = [nat[pl.ds(v * count + place, rows), :] for v in range(variables)]
            for k in range(g * group_members, (g + 1) * group_members):
                total = perturb[k, 0, pl.ds(place, rows), :].astype(f32) * slopes[0]
                for v in range(1, variables):
                    total = total + perturb[k, v, pl.ds(place, rows), :].astype(f32) * slopes[v]
                field[pl.ds(k * count + place, rows), :] = total * kappa[...]

        for y in range(rows):
            block = field[pl.ds(g * group_rows + y, lanes, stride=rows), :]
            pack_row(dims, ring.at[g], rows_out.at[g, 0], rows_out.at[g, 1], y, block.T)
        if g == 0:
            wait_around()
        moves[g][0]()
    mix[...] = stacked_weights(static_weight * static_blocks(static_vert, levels).T)
    load_chi.wait()
    for y in range(rows):
        line = pl.ds(y, column, stride=rows)
        out_chi[line, :] = chi[line, :] + mixed(mix, grad[y], 1)
    mix[...] = stacked_weights(vertical_blocks(bounds, lanes, levels, True))
    load_alpha.wait()
    inverse = 1.0 / kappa[...]
    for g in range(groups):
        moves[g][1]()
        fill_halo_rows(
            dims, ring.at[g], lambda d: rows_in[g, 0, d].astype(f32),
            lambda d: rows_in[g, 1, d].astype(f32),
        )
        diffuse(dims, ring.at[g], work, kap)
        for y in range(rows):
            line = pl.ds(g * group_rows + y, lanes, stride=rows)
            out_alpha[line, :] = alpha[line, :] + inverse[y : y + 1] * mixed(
                mix, ring[g, depth + y, inner], 1
            )


def observe_kernel(
    rows, band, padded, count_ref, table_ref, anchor_ref, weight_ref, background_ref, observed_ref,
    inv_var_ref, jacobian_ref, out_ref, high_ref, low_ref,
):
    places = anchor_ref.shape[1]
    anchor = anchor_ref[...]
    anchor_row = anchor // band
    anchor_col = anchor - anchor_row * band
    slot = lax.broadcasted_iota(jnp.int32, (padded, places), 0)
    at_left = slot == anchor_col
    at_right = slot == anchor_col + 1
    total = background_ref[...].astype(f32).T
    for y in range(rows):
        upper = anchor_row == y
        lower = anchor_row == y - 1
        zero = jnp.zeros(anchor.shape, f32)
        left = jnp.where(upper, weight_ref[0:1], jnp.where(lower, weight_ref[2:3], zero))
        right = jnp.where(upper, weight_ref[1:2], jnp.where(lower, weight_ref[3:4], zero))
        weights = jnp.where(at_left, left, jnp.where(at_right, right, 0.0))
        high, low = split(weights)
        high_ref[y] = high
        low_ref[y] = low
        cells = table_ref[y]
        total = total + lax.dot_general(cells, high, TN, preferred_element_type=f32)
        total = total + lax.dot_general(cells, low, TN, preferred_element_type=f32)
    bent = jnp.tanh(total)
    modeled = jnp.dot(jacobian_ref[...], bent, precision=highest, preferred_element_type=f32)
    position = lax.broadcasted_iota(jnp.int32, modeled.shape, 1)
    misfit = jnp.where(
        position < count_ref[0], (modeled - observed_ref[...]) * inv_var_ref[...], 0.0
    )
    back = lax.dot_general(
        jacobian_ref[...], misfit, TN, precision=highest, preferred_element_type=f32
    )
    state_high, state_low = split((1.0 - bent * bent) * back)
    for y in range(rows):
        high = high_ref[y]
        cells = lax.dot_general(high, state_high, NT, preferred_element_type=f32)
        cells = cells + lax.dot_general(low_ref[y], state_high, NT, preferred_element_type=f32)
        cells = cells + lax.dot_general(high, state_low, NT, preferred_element_type=f32)
        out_ref[y] = cells


def choose(index, options):
    result = options[0]
    for place in range(1, len(options)):
        result = jnp.where(index == place, options[place], result)
    return result


def body(
    alpha, perturb, chi, kappa, vert_bounds, static_vert, fine_owner, obs_stencil, obs_weight,
    background, observed, inv_var, jacobian, obs_count,
):
    members, levels, rows, width = alpha.shape
    variables = perturb.shape[1]
    column = variables * levels
    depth = NDIFF
    groups = lax.axis_size("mem")
    band = width // groups
    shift = band // 2
    rim = shift + 1
    me = lax.axis_index("mem")
    count = rows * levels
    places = obs_stencil.shape[0]
    dims = (rows, levels, width, variables, depth)
    ens_scale = ensemble_weight / math.sqrt(members * groups - 1)
    owners = fine_owner[0]
    band_ids = lax.iota(jnp.int32, groups)

    def band_of(group):
        return jnp.sum(jnp.where(owners == group, band_ids, 0))

    smem = pl.BlockSpec(memory_space=pltpu.SMEM)
    vmem = pl.BlockSpec(memory_space=pltpu.VMEM)
    hbm = pl.BlockSpec(memory_space=pl.ANY)
    lanes = column
    grouped = members * levels // lanes
    ring_rows, ring_width = rows + 2 * depth, width + 4 * SIDE
    alpha_flat = alpha.reshape(members * count, width)
    chi_flat = chi.reshape(variables * count, width)
    perturb_flat = perturb.reshape(members, variables, count, width)

    def exchange_scratch(extra):
        return [
            pltpu.VMEM((grouped, 2, depth, width, lanes), bf16),
            pltpu.VMEM((grouped, 2, depth, width, lanes), bf16),
        ] + extra

    tile_scratch = [
        pltpu.VMEM((members * count, width), f32),
        pltpu.VMEM((variables * count, width), f32),
        pltpu.VMEM((members, variables, count, width), bf16),
        pltpu.VMEM((grouped, ring_rows, ring_width, lanes), f32),
        pltpu.VMEM((ring_rows, ring_width, lanes), f32),
    ]
    partial, kap = pl.pallas_call(
        lambda *refs: forward_kernel(dims, ens_scale, *refs),
        in_specs=[vmem, vmem, vmem, hbm, hbm, hbm],
        out_specs=[vmem, vmem],
        out_shape=[
            jax.ShapeDtypeStruct((rows, width, column), f32),
            jax.ShapeDtypeStruct((ring_rows, ring_width, lanes), f32),
        ],
        scratch_shapes=tile_scratch + exchange_scratch([
            pltpu.VMEM((2, SIDE, width), f32),
            pltpu.VMEM((members * count, width), f32),
            pltpu.VMEM((variables * count, width), f32),
            pltpu.VMEM((rows, column, width), f32),
            pltpu.VMEM((2 * lanes, 2 * lanes), bf16),
            pltpu.SemaphoreType.DMA((grouped + 2,)),
            pltpu.SemaphoreType.DMA((grouped + 1, 8)),
            pltpu.SemaphoreType.DMA((grouped + 1, 8)),
        ]),
        compiler_params=pltpu.CompilerParams(
            collective_id=0, has_side_effects=True, vmem_limit_bytes=40 << 20
        ),
        name="forward",
    )(vert_bounds, static_vert, kappa, alpha_flat, chi_flat, perturb_flat)

    own_band = band_of(me)
    east_rim = shifted(partial[:, :rim].astype(bf16), "gx", -1)
    near = [partial[:, b * band + shift : (b + 1) * band] for b in range(groups)]
    far = [partial[:, b * band : b * band + rim] for b in range(1, groups)]
    far.append(east_rim.astype(f32))
    halves = []
    for parts in (near, far):
        half = choose(own_band, parts)
        for hop in range(1, groups):
            away = choose(band_of((me + hop) % groups), parts).astype(bf16)
            half = half + shifted(away, "mem", hop).astype(f32)
        halves.append(half)
    increment = jnp.concatenate(halves, axis=1)
    padded = -(-(band + 1) // 16) * 16
    table = jnp.pad(increment.astype(bf16), ((0, 0), (0, padded - band - 1), (0, 0)))

    region_grad = pl.pallas_call(
        lambda *refs: observe_kernel(rows, band, padded, *refs),
        in_specs=[smem] + [vmem] * 7,
        out_specs=vmem,
        out_shape=jax.ShapeDtypeStruct((rows, padded, column), f32),
        scratch_shapes=[
            pltpu.VMEM((rows, padded, places), bf16),
            pltpu.VMEM((rows, padded, places), bf16),
        ],
        compiler_params=params(),
        name="observe",
    )(
        obs_count, table, obs_stencil.reshape(1, places), obs_weight, background, observed,
        inv_var, jacobian,
    )

    near, far = region_grad[:, : band - shift], region_grad[:, band - shift : band + 1]
    far_pieces = [(own_band, far)]
    for hop in range(1, groups):
        far_pieces.append((band_of((me - hop) % groups), shifted(far, "mem", hop)))
    rim_grad = choose_equal(groups - 1, far_pieces)
    near, rim_grad = lax.optimization_barrier((near, rim_grad))
    west_rim = shifted(rim_grad, "gx", 1)
    near_pieces = [(own_band, near)]
    for hop in range(1, groups):
        near_pieces.append((band_of((me - hop) % groups), shifted(near, "mem", hop)))
    grad_cells = jnp.pad(west_rim, ((0, 0), (0, width - rim), (0, 0)))
    for b in range(groups):
        before = b * band + shift
        grad_cells = grad_cells + jnp.pad(
            choose_equal(b, near_pieces), ((0, 0), (before, width - (b + 1) * band), (0, 0))
        )
    for b in range(1, groups):
        before = b * band
        grad_cells = grad_cells + jnp.pad(
            choose_equal(b - 1, far_pieces), ((0, 0), (before, width - before - rim), (0, 0))
        )

    grad_alpha, grad_chi = pl.pallas_call(
        lambda *refs: backward_kernel(dims, ens_scale, *refs),
        in_specs=[vmem, vmem, vmem, vmem, vmem, hbm, hbm, hbm],
        out_specs=[vmem, vmem],
        out_shape=[
            jax.ShapeDtypeStruct((members * count, width), f32),
            jax.ShapeDtypeStruct((variables * count, width), f32),
        ],
        scratch_shapes=tile_scratch + exchange_scratch([
            pltpu.VMEM((members * count, width), f32),
            pltpu.VMEM((variables * count, width), f32),
            pltpu.VMEM((2 * lanes, 2 * lanes), bf16),
            pltpu.SemaphoreType.DMA((grouped + 2,)),
            pltpu.SemaphoreType.DMA((grouped, 8)),
            pltpu.SemaphoreType.DMA((grouped, 8)),
        ]),
        compiler_params=pltpu.CompilerParams(
            collective_id=1, has_side_effects=True, vmem_limit_bytes=40 << 20
        ),
        name="backward",
    )(vert_bounds, static_vert, kappa, grad_cells, kap, alpha_flat, chi_flat, perturb_flat)
    return grad_alpha.reshape(alpha.shape), grad_chi.reshape(chi.shape)


def choose_equal(wanted, pieces):
    result = pieces[0][1]
    for index, piece in pieces[1:]:
        result = jnp.where(index == wanted, piece, result)
    return result


def solution(mesh):
    in_specs = (
        P("mem", None, "gy", "gx"),
        P("mem", None, None, "gy", "gx"),
        P(None, None, "gy", "gx"),
        P("gy", "gx"),
        P(),
        P(),
        P(("gy", "gx"), None),
        P(("mem", "gy", "gx")),
        P(None, ("mem", "gy", "gx")),
        P(("mem", "gy", "gx"), None),
        P(None, ("mem", "gy", "gx")),
        P(None, ("mem", "gy", "gx")),
        P(),
        P(("mem", "gy", "gx")),
    )
    out_specs = (P("mem", None, "gy", "gx"), P(None, None, "gy", "gx"))
    return jax.shard_map(body, mesh=mesh, in_specs=in_specs, out_specs=out_specs, check_vma=False)
```

profile of v0, /device:TPU:0, one launch (start us, length us, event | category | flops | bytes accessed | tf_op | source)
XLA Modules:
  0.0 86.9 jit_solution(13041547853646487719)
XLA Ops:
  0.6 2.2 %copy-done = bf16[8,4,32,16,128]{4,3,2,1,0:T(8,128)(2,1)S(1)} copy-done((bf16[8,4,32,16,128]{4,3,2,1,0:T(8,128)(2,1)S(1)}, bf16[8,4,32,16,128]{4,3,2,1,0:T(8,128)(2,1)}, u32[]{:S(2)}) %copy-start) | copy-done | bytes 4194328
  2.8 1.6 %copy-done.2 = f32[8,32,16,128]{3,2,1,0:T(8,128)S(1)} copy-done((f32[8,32,16,128]{3,2,1,0:T(8,128)S(1)}, f32[8,32,16,128]{3,2,1,0:T(8,128)}, u32[]{:S(2)}) %copy-start.2) | copy-done | bytes 2097176
  4.4 1.2 %copy-done.4 = f32[4,32,16,128]{3,2,1,0:T(8,128)S(1)} copy-done((f32[4,32,16,128]{3,2,1,0:T(8,128)S(1)}, f32[4,32,16,128]{3,2,1,0:T(8,128)}, u32[]{:S(2)}) %copy-start.4) | copy-done | bytes 1048600
  5.6 0.8 copy-done.8
  6.5 0.7 copy-done.10
  7.2 0.7 copy-done.12
  7.9 18.8 %forward.1 = (f32[16,128,128]{2,1,0:T(8,128)S(1)}, f32[24,160,128]{2,1,0:T(8,128)S(1)}) custom-call(s32[2,32]{1,0:T(2,128)S(1)} %copy-done.12, f32[4,32,32]{2,1,0:T(8,128)S(1)} %copy-done.8, f32[16,128]{1,0:T(8,128)S(1)} %copy-done.10, f32[4096,128]{1,0:T(8,128)S(1)} %bitcast.20, f32[2048,128]{1,0:T(8,128)S(1)} %bitcast.22, bf16[8,4,512,128]{3,2,1,0:T(8,128)(2,1)S(1)} %bitcast.18), custom_call_target="tpu_custom_call" | custom-call | tf_op jit(solution)/shard_map/forward/pallas_call | solution.py:514
  26.6 0.0 copy-start.6
  26.6 1.3 %copy-done.6 = f32[24,160,128]{2,1,0:T(8,128)} copy-done((f32[24,160,128]{2,1,0:T(8,128)}, f32[24,160,128]{2,1,0:T(8,128)S(1)}, u32[]{:S(2)}) %copy-start.6) | copy-done | bytes 1966104
  27.9 1.0 %collective-permute-start.1 = (bf16[16,33,128]{2,1,0:T(8,128)(2,1)S(1)}, bf16[16,33,128]{2,1,0:T(8,128)(2,1)S(1)}, u32[]{:S(2)}, u32[]{:S(2)}) collective-permute-start(bf16[16,33,128]{2,1,0:T(8,128)(2,1)S(1)} %slice.37), channel_id=1, source_target_pairs={{0,3},{1,0},{2,1},{3,2},{4,7},{5,4},{6,5},{7,6},{8,11},{9,8},{10,9... | collective-permute-start | bytes 405512 | tf_op jit(solution)/shard_map/ppermute | solution.py:25
  28.9 0.7 fusion.8
  30.2 1.6 %collective-permute-start = (bf16[16,32,128]{2,1,0:T(8,128)(2,1)S(1)}, bf16[16,32,128]{2,1,0:T(8,128)(2,1)S(1)}, u32[]{:S(2)}, u32[]{:S(2)}) collective-permute-start(bf16[16,32,128]{2,1,0:T(8,128)(2,1)S(1)} %select_convert_fusion), channel_id=1, source_target_pairs={{0,16},{16,0},{1,17},{17,1},{2,18},{18,2},{3,19},{19,3},{4,20},{20... | collective-permute-start | bytes 393224 | tf_op jit(solution)/shard_map/ppermute | solution.py:25
  33.1 0.6 collective-permute-start.2
  33.7 1.6 %collective-permute-done = bf16[16,32,128]{2,1,0:T(8,128)(2,1)S(1)} collective-permute-done((bf16[16,32,128]{2,1,0:T(8,128)(2,1)S(1)}, bf16[16,32,128]{2,1,0:T(8,128)(2,1)S(1)}, u32[]{:S(2)}, u32[]{:S(2)}) %collective-permute-start) | collective-permute-done | bytes 131104 | tf_op jit(solution)/shard_map/ppermute | solution.py:25
  35.2 0.1 add_convert_fusion
  35.3 3.5 %collective-permute-done.2 = bf16[16,33,128]{2,1,0:T(8,128)(2,1)S(1)} collective-permute-done((bf16[16,33,128]{2,1,0:T(8,128)(2,1)S(1)}, bf16[16,33,128]{2,1,0:T(8,128)(2,1)S(1)}, u32[]{:S(2)}, u32[]{:S(2)}) %collective-permute-start.2) | collective-permute-done | bytes 135200 | tf_op jit(solution)/shard_map/ppermute | solution.py:25
  38.8 0.1 fusion.3
  38.8 0.7 fusion.5.refs_1_
  39.6 9.6 %observe.1 = f32[16,80,128]{2,1,0:T(8,128)} custom-call(s32[1]{0:T(128)S(6)} %copy.18.refs_0_, bf16[16,80,128]{2,1,0:T(8,128)(2,1)} %fusion.5.refs_1_, s32[1,1024]{1,0:T(1,128)} %bitcast.26, f32[4,1024]{1,0:T(4,128)} %refs_3_.1, bf16[1024,128]{1,0:T(8,128)(2,1)} %refs_4_.1, f32[8,1024]{1,0:T(8,128)} %refs_5_.1, f32[8,1024]{1,0:T(8,128)} %refs_6_.1, ...), custom_call_target="tpu_custom_call" | custom-call | tf_op jit(solution)/shard_map/observe/pallas_call | solution.py:554
  49.2 1.0 %slice.27 = f32[16,33,128]{2,1,0:T(8,128)S(1)} slice(f32[16,80,128]{2,1,0:T(8,128)} %observe.1), slice={[0:16], [32:65], [0:128]} | slice | bytes 540672 | tf_op jit(solution)/shard_map/slice | solution.py:570
  50.2 1.5 %collective-permute-start.3 = (f32[16,33,128]{2,1,0:T(8,128)S(1)}, f32[16,33,128]{2,1,0:T(8,128)}, u32[]{:S(2)}, u32[]{:S(2)}) collective-permute-start(f32[16,33,128]{2,1,0:T(8,128)S(1)} %slice.27), channel_id=1, source_target_pairs={{0,16},{16,0},{1,17},{17,1},{2,18},{18,2},{3,19},{19,3},{4,20},{20... | collective-permute-start | bytes 811016 | tf_op jit(solution)/shard_map/ppermute | solution.py:25
  53.1 1.0 %slice.26 = f32[16,32,128]{2,1,0:T(8,128)S(1)} slice(f32[16,80,128]{2,1,0:T(8,128)} %observe.1), slice={[0:16], [0:32], [0:128]} | slice | bytes 524288 | tf_op jit(solution)/shard_map/slice | solution.py:570
  54.1 5.2 %collective-permute-done.3 = f32[16,33,128]{2,1,0:T(8,128)} collective-permute-done((f32[16,33,128]{2,1,0:T(8,128)S(1)}, f32[16,33,128]{2,1,0:T(8,128)}, u32[]{:S(2)}, u32[]{:S(2)}) %collective-permute-start.3) | collective-permute-done | bytes 270368 | tf_op jit(solution)/shard_map/ppermute | solution.py:25
  59.3 1.1 %broadcast_select_fusion.1 = (f32[16,33,128]{2,1,0:T(8,128)S(1)}, f32[16,33,128]{2,1,0:T(8,128)S(1)}) fusion(f32[16,33,128]{2,1,0:T(8,128)} %collective-permute-done.3, pred[]{:T(512)S(6)} %eq.63, f32[16,80,128]{2,1,0:T(8,128)} %observe.1, pred[]{:T(512)S(6)} %eq.64), kind=kLoop, calls=%fused_computation.14 | loop fusion | flops 135168 | bytes 1081346 | tf_op jit(solution)/shard_map/jit(_where)/select_n | solution.py:619
  60.5 1.8 %collective-permute-start.5 = (f32[16,32,128]{2,1,0:T(8,128)S(1)}, f32[16,32,128]{2,1,0:T(8,128)S(1)}, u32[]{:S(2)}, u32[]{:S(2)}) collective-permute-start(f32[16,32,128]{2,1,0:T(8,128)S(1)} %slice.26), channel_id=1, source_target_pairs={{0,16},{16,0},{1,17},{17,1},{2,18},{18,2},{3,19},{19,3},{4,20},{20... | collective-permute-start | bytes 786440 | tf_op jit(solution)/shard_map/ppermute | solution.py:25
  62.3 5.2 %collective-permute-done.5 = f32[16,32,128]{2,1,0:T(8,128)S(1)} collective-permute-done((f32[16,32,128]{2,1,0:T(8,128)S(1)}, f32[16,32,128]{2,1,0:T(8,128)S(1)}, u32[]{:S(2)}, u32[]{:S(2)}) %collective-permute-start.5) | collective-permute-done | bytes 262176 | tf_op jit(solution)/shard_map/ppermute | solution.py:25
  67.6 1.2 %collective-permute-done.4 = f32[16,33,128]{2,1,0:T(8,128)S(1)} collective-permute-done((f32[16,33,128]{2,1,0:T(8,128)S(1)}, f32[16,33,128]{2,1,0:T(8,128)S(1)}, u32[]{:S(2)}, u32[]{:S(2)}) %collective-permute-start.4) | collective-permute-done | bytes 270368 | tf_op jit(solution)/shard_map/ppermute | solution.py:25
  68.8 0.1 pad_add_fusion.refs_3_
  68.9 1.5 %copy-done.7 = f32[24,160,128]{2,1,0:T(8,128)S(1)} copy-done((f32[24,160,128]{2,1,0:T(8,128)S(1)}, f32[24,160,128]{2,1,0:T(8,128)}, u32[]{:S(2)}) %copy-start.7) | copy-done | bytes 1966104
  70.5 14.1 %backward.1 = (f32[4096,128]{1,0:T(8,128)S(1)}, f32[2048,128]{1,0:T(8,128)S(1)}) custom-call(s32[2,32]{1,0:T(2,128)S(1)} %copy-done.13, f32[4,32,32]{2,1,0:T(8,128)S(1)} %copy-done.9, f32[16,128]{1,0:T(8,128)S(1)} %copy-done.11, f32[16,128,128]{2,1,0:T(8,128)S(1)} %pad_add_fusion.refs_3_, f32[24,160,128]{2,1,0:T(8,128)S(1)} %copy-done.7, ...), custom_call_target="tpu_custom_call" | custom-call | tf_op jit(solution)/shard_map/backward/pallas_call | solution.py:592
  84.6 1.3 %copy.19 = f32[8,32,16,128]{3,2,1,0:T(8,128)} copy(f32[8,32,16,128]{3,2,1,0:T(8,128)S(1)} %bitcast.24) | data formatting | bytes 4194304
  85.9 1.0 %copy.20 = f32[4,32,16,128]{3,2,1,0:T(8,128)} copy(f32[4,32,16,128]{3,2,1,0:T(8,128)S(1)} %bitcast.25) | data formatting | bytes 2097152
  (27 shorter events, 0.2 us)
Async XLA Ops:
  0.6 2.2 %copy-start = (bf16[8,4,32,16,128]{4,3,2,1,0:T(8,128)(2,1)S(1)}, bf16[8,4,32,16,128]{4,3,2,1,0:T(8,128)(2,1)}, u32[]{:S(2)}) copy-start(bf16[8,4,32,16,128]{4,3,2,1,0:T(8,128)(2,1)} %param.15) | copy-start | bytes 12582916
  2.8 1.6 %copy-start.2 = (f32[8,32,16,128]{3,2,1,0:T(8,128)S(1)}, f32[8,32,16,128]{3,2,1,0:T(8,128)}, u32[]{:S(2)}) copy-start(f32[8,32,16,128]{3,2,1,0:T(8,128)} %param.14) | copy-start | bytes 6291460
  4.4 1.2 %copy-start.4 = (f32[4,32,16,128]{3,2,1,0:T(8,128)S(1)}, f32[4,32,16,128]{3,2,1,0:T(8,128)}, u32[]{:S(2)}) copy-start(f32[4,32,16,128]{3,2,1,0:T(8,128)} %param.16) | copy-start | bytes 3145732
  5.6 0.8 copy-start.8
  6.5 0.7 copy-start.10
  7.2 0.7 copy-start.12
  7.9 21.0 %copy-start.14 = (s32[1,2]{1,0:T(1,128)S(1)}, s32[1,2]{1,0:T(1,128)}, u32[]{:S(2)}) copy-start(s32[1,2]{1,0:T(1,128)} %param.20) | copy-start | bytes 28
  26.6 1.3 %copy-start.6 = (f32[24,160,128]{2,1,0:T(8,128)}, f32[24,160,128]{2,1,0:T(8,128)S(1)}, u32[]{:S(2)}) copy-start(f32[24,160,128]{2,1,0:T(8,128)S(1)} %get-tuple-element.11.refs_4_) | copy-start | bytes 5898244
  27.9 5.1 %collective-permute-start.1 = (bf16[16,33,128]{2,1,0:T(8,128)(2,1)S(1)}, bf16[16,33,128]{2,1,0:T(8,128)(2,1)S(1)}, u32[]{:S(2)}, u32[]{:S(2)}) collective-permute-start(bf16[16,33,128]{2,1,0:T(8,128)(2,1)S(1)} %slice.37), channel_id=1, source_target_pairs={{0,3},{1,0},{2,1},{3,2},{4,7},{5,4},{6,5},{7,6},{8,11},{9,8},{10,9... | collective-permute-start | bytes 405512 | tf_op jit(solution)/shard_map/ppermute | solution.py:25
  30.2 5.1 %collective-permute-start = (bf16[16,32,128]{2,1,0:T(8,128)(2,1)S(1)}, bf16[16,32,128]{2,1,0:T(8,128)(2,1)S(1)}, u32[]{:S(2)}, u32[]{:S(2)}) collective-permute-start(bf16[16,32,128]{2,1,0:T(8,128)(2,1)S(1)} %select_convert_fusion), channel_id=1, source_target_pairs={{0,16},{16,0},{1,17},{17,1},{2,18},{18,2},{3,19},{19,3},{4,20},{20... | collective-permute-start | bytes 393224 | tf_op jit(solution)/shard_map/ppermute | solution.py:25
  33.1 5.7 %collective-permute-start.2 = (bf16[16,33,128]{2,1,0:T(8,128)(2,1)S(1)}, bf16[16,33,128]{2,1,0:T(8,128)(2,1)S(1)}, u32[]{:S(2)}, u32[]{:S(2)}) collective-permute-start(bf16[16,33,128]{2,1,0:T(8,128)(2,1)S(1)} %fusion.4), channel_id=1, source_target_pairs={{0,16},{16,0},{1,17},{17,1},{2,18},{18,2},{3,19},{19,3},{4,20},{20... | collective-permute-start | bytes 405512 | tf_op jit(solution)/shard_map/ppermute | solution.py:25
  38.8 30.0 %copy-start.5 = (f32[4,32,16,128]{3,2,1,0:T(8,128)S(1)}, f32[4,32,16,128]{3,2,1,0:T(8,128)}, u32[]{:S(2)}) copy-start(f32[4,32,16,128]{3,2,1,0:T(8,128)} %param.16) | copy-start | bytes 3145732
  39.6 29.3 %copy-start.3 = (f32[8,32,16,128]{3,2,1,0:T(8,128)S(1)}, f32[8,32,16,128]{3,2,1,0:T(8,128)}, u32[]{:S(2)}) copy-start(f32[8,32,16,128]{3,2,1,0:T(8,128)} %param.14) | copy-start | bytes 6291460
  50.2 9.2 %collective-permute-start.3 = (f32[16,33,128]{2,1,0:T(8,128)S(1)}, f32[16,33,128]{2,1,0:T(8,128)}, u32[]{:S(2)}, u32[]{:S(2)}) collective-permute-start(f32[16,33,128]{2,1,0:T(8,128)S(1)} %slice.27), channel_id=1, source_target_pairs={{0,16},{16,0},{1,17},{17,1},{2,18},{18,2},{3,19},{19,3},{4,20},{20... | collective-permute-start | bytes 811016 | tf_op jit(solution)/shard_map/ppermute | solution.py:25
  54.1 14.8 %copy-start.1 = (bf16[8,4,32,16,128]{4,3,2,1,0:T(8,128)(2,1)S(1)}, bf16[8,4,32,16,128]{4,3,2,1,0:T(8,128)(2,1)}, u32[]{:S(2)}) copy-start(bf16[8,4,32,16,128]{4,3,2,1,0:T(8,128)(2,1)} %param.15) | copy-start | bytes 12582916
  54.1 14.8 %copy-start.9 = (f32[4,32,32]{2,1,0:T(8,128)S(1)}, f32[4,32,32]{2,1,0:T(8,128)}, u32[]{:S(2)}) copy-start(f32[4,32,32]{2,1,0:T(8,128)} %refs_1_.3) | copy-start | bytes 49156
  54.1 14.8 %copy-start.11 = (f32[16,128]{1,0:T(8,128)S(1)}, f32[16,128]{1,0:T(8,128)}, u32[]{:S(2)}) copy-start(f32[16,128]{1,0:T(8,128)} %refs_2_.3) | copy-start | bytes 24580
  54.1 14.8 %copy-start.13 = (s32[2,32]{1,0:T(2,128)S(1)}, s32[2,32]{1,0:T(2,128)}, u32[]{:S(2)}) copy-start(s32[2,32]{1,0:T(2,128)} %refs_0_.4) | copy-start | bytes 772
  60.5 7.0 %collective-permute-start.5 = (f32[16,32,128]{2,1,0:T(8,128)S(1)}, f32[16,32,128]{2,1,0:T(8,128)S(1)}, u32[]{:S(2)}, u32[]{:S(2)}) collective-permute-start(f32[16,32,128]{2,1,0:T(8,128)S(1)} %slice.26), channel_id=1, source_target_pairs={{0,16},{16,0},{1,17},{17,1},{2,18},{18,2},{3,19},{19,3},{4,20},{20... | collective-permute-start | bytes 786440 | tf_op jit(solution)/shard_map/ppermute | solution.py:25
  62.3 6.5 %collective-permute-start.4 = (f32[16,33,128]{2,1,0:T(8,128)S(1)}, f32[16,33,128]{2,1,0:T(8,128)S(1)}, u32[]{:S(2)}, u32[]{:S(2)}) collective-permute-start(f32[16,33,128]{2,1,0:T(8,128)S(1)} %get-tuple-element.9), channel_id=1, source_target_pairs={{0,1},{1,2},{2,3},{3,0},{4,5},{5,6},{6,7},{7,4},{8,9},{9,10},{10,1... | collective-permute-start | bytes 811016 | tf_op jit(solution)/shard_map/ppermute | solution.py:25
  68.9 1.5 %copy-start.7 = (f32[24,160,128]{2,1,0:T(8,128)S(1)}, f32[24,160,128]{2,1,0:T(8,128)}, u32[]{:S(2)}) copy-start(f32[24,160,128]{2,1,0:T(8,128)} %copy-done.6) | copy-start | bytes 5898244
where the time goes:
time: 87.7 us; the launch traced here: 86.9 us
  Pallas kernels  42.4 us (48%)
  waiting for transfers between devices  16.7 us (19%)
  local copies, waits for them, and re-layouts  14.3 us (16%)
  starting transfers between devices  6.46 us (7%)
  between operations  4.05 us (5%)
  other arithmetic  2.88 us (3%)
    pallas_call x1, Pallas kernels, body(): pl.pallas_call(lambda *refs: forward_kernel(dims, ens_scale, *refs), in_s...  18.8 us
    ppermute x6, waiting for transfers between devices, shifted(): return lax.ppermute(value, axis, pairs)  16.7 us
    pallas_call x1, Pallas kernels, body(): pl.pallas_call(lambda *refs: backward_kernel(dims, ens_scale, *refs), in_...  14.1 us
    unnamed x32, local copies, waits for them, and re-layouts  12.3 us
    pallas_call x1, Pallas kernels, body(): pl.pallas_call(lambda *refs: observe_kernel(rows, band, padded, *refs), i...  9.6 us
    ppermute x6, starting transfers between devices, shifted(): return lax.ppermute(value, axis, pairs)  6.46 us
  transfers between devices with their start and end apart: 6, of which 5 were waited for; matrix products, arithmetic and copies ran while one was open for 2% of the time, Pallas kernels for 0%

commit v1 on v0

v1 whole, which is shorter than its diff:
```python
import math

import jax
import jax.numpy as jnp
from jax import lax
from jax.experimental import pallas as pl
from jax.experimental.pallas import tpu as pltpu
from jax.sharding import PartitionSpec as P

NDIFF = 4

ensemble_weight = 0.8
static_weight = 0.6
vertical_scale = 2.0
code_limit = 32767.0
f32 = jnp.float32
bf16 = jnp.bfloat16
SIDE = 8
NN = (((1,), (0,)), ((), ()))
NT = (((1,), (1,)), ((), ()))
TN = (((0,), (0,)), ((), ()))


def compass():
    gx, gy = lax.axis_index("gx"), lax.axis_index("gy")
    gx_count, gy_count = lax.axis_size("gx"), lax.axis_size("gy")
    east, west = lax.rem(gx + 1, gx_count), lax.rem(gx + gx_count - 1, gx_count)
    return east, west, gy - 1, gy + 1, gy > 0, gy < gy_count - 1


def greet_around(partners):
    east, west, north, south, has_north, has_south = compass()
    barrier = pltpu.get_barrier_semaphore()

    def greet(device):
        pl.semaphore_signal(
            barrier, inc=1, device_id=device, device_id_type=pl.DeviceIdType.MESH
        )

    for device in [{"gx": east}, {"gx": west}] + partners:
        greet(device)

    @pl.when(has_north)
    def _():
        for device in ({"gy": north}, {"gy": north, "gx": east}, {"gy": north, "gx": west}):
            greet(device)

    @pl.when(has_south)
    def _():
        for device in ({"gy": south}, {"gy": south, "gx": east}, {"gy": south, "gx": west}):
            greet(device)


def wait_around(partners):
    east, west, north, south, has_north, has_south = compass()
    peers = partners + 2 + 3 * has_north.astype(jnp.int32) + 3 * has_south.astype(jnp.int32)
    pl.semaphore_wait(pltpu.get_barrier_semaphore(), peers)


def ring_copies(dims, ring, first_rows, last_rows, south_in, north_in, send, recv):
    rows, levels, width, variables, depth = dims
    east, west, north, south, has_north, has_south = compass()
    top, bottom = pl.ds(depth, depth), pl.ds(rows, depth)
    body, above, below = pl.ds(depth, rows), pl.ds(0, depth), pl.ds(depth + rows, depth)
    first, last = pl.ds(2 * SIDE, SIDE), pl.ds(SIDE + width, SIDE)
    before, after = pl.ds(SIDE, SIDE), pl.ds(2 * SIDE + width, SIDE)

    def copy(source, target, place, device):
        return pltpu.make_async_remote_copy(
            src_ref=source, dst_ref=target, send_sem=send.at[place], recv_sem=recv.at[place],
            device_id=device, device_id_type=pl.DeviceIdType.MESH,
        )

    across = [
        copy(ring.at[body, last], ring.at[body, before], 0, {"gx": east}),
        copy(ring.at[body, first], ring.at[body, after], 1, {"gx": west}),
    ]
    up = [
        copy(first_rows, south_in, 2, {"gy": north}),
        copy(ring.at[top, last], ring.at[below, before], 3, {"gy": north, "gx": east}),
        copy(ring.at[top, first], ring.at[below, after], 4, {"gy": north, "gx": west}),
    ]
    down = [
        copy(last_rows, north_in, 5, {"gy": south}),
        copy(ring.at[bottom, last], ring.at[above, before], 6, {"gy": south, "gx": east}),
        copy(ring.at[bottom, first], ring.at[above, after], 7, {"gy": south, "gx": west}),
    ]

    def start():
        @pl.when(has_north)
        def _():
            for item in up:
                item.start()

        @pl.when(has_south)
        def _():
            for item in down:
                item.start()

        for item in across:
            item.start()

    def wait():
        for item in across:
            item.wait_recv()
            item.wait_send()

        @pl.when(has_north)
        def _():
            for item in down:
                item.wait_recv()
            for item in up:
                item.wait_send()

        @pl.when(has_south)
        def _():
            for item in up:
                item.wait_recv()
            for item in down:
                item.wait_send()

    return start, wait


def fill_halo_rows(dims, ring, from_south, from_north):
    rows, levels, width, variables, depth = dims
    east, west, north, south, has_north, has_south = compass()
    inner, whole = pl.ds(2 * SIDE, width), pl.ds(SIDE, width + 2 * SIDE)

    @pl.when(has_south)
    def _():
        for d in range(depth):
            ring[depth + rows + d, inner] = from_south(d)

    @pl.when(jnp.logical_not(has_south))
    def _():
        for d in range(depth):
            ring[depth + rows + d, whole] = ring[depth + rows - 1 - d, whole]

    @pl.when(has_north)
    def _():
        for d in range(depth):
            ring[d, inner] = from_north(d)

    @pl.when(jnp.logical_not(has_north))
    def _():
        for d in range(depth):
            ring[d, whole] = ring[2 * depth - 1 - d, whole]


def diffuse(dims, ring, work, kap):
    rows, levels, width, variables, depth = dims
    for step in range(1, depth + 1):
        source, target = (ring, work) if step % 2 else (work, ring)
        start, stop = (SIDE, width + 3 * SIDE) if step < depth else (2 * SIDE, width + 2 * SIDE)

        @pl.loop(0, rows // 2 + depth - step)
        def _(pair, source=source, target=target, start=start, stop=stop, step=step):
            y = step + 2 * pair
            for x in range(start, stop, 6 * SIDE):
                size = min(6 * SIDE, stop - x)
                here = pl.ds(x, size)
                held = [source[y + i, here] for i in (-1, 0, 1, 2)]
                for i in (0, 1):
                    center = held[i + 1]
                    sides = source[y + i, pl.ds(x - 1, size)] + source[y + i, pl.ds(x + 1, size)]
                    change = (held[i] + held[i + 2]) + sides - 4.0 * center
                    target[y + i, here] = center + kap[y + i, here] * change


def split(value):
    high = value.astype(bf16)
    return high, (value - high.astype(f32)).astype(bf16)


def stacked_weights(weights):
    high, low = split(weights)
    return jnp.concatenate(
        [
            jnp.concatenate([high, high], axis=1),
            jnp.concatenate([low, jnp.zeros_like(low)], axis=1),
        ],
        axis=0,
    )


def mixed(weights_ref, value, axis):
    half = weights_ref.shape[0] // 2
    numbers = NT if axis else NN
    both = lax.dot_general(
        weights_ref[...], jnp.concatenate(split(value), axis=axis), numbers,
        preferred_element_type=f32,
    )
    return both[:half] + both[half:]


def lane_grid(lanes, levels):
    row = lax.broadcasted_iota(jnp.int32, (lanes, lanes), 0)
    col = lax.broadcasted_iota(jnp.int32, (lanes, lanes), 1)
    row_block, col_block = row // levels, col // levels
    return row - row_block * levels, col - col_block * levels, row_block == col_block


def vertical_blocks(bounds_ref, lanes, levels, transposed):
    row, col, same = lane_grid(lanes, levels)
    bounds = bounds_ref[...].astype(f32)
    limits = []
    for side in range(2):
        line = jnp.concatenate([bounds[side : side + 1]] * (lanes // levels), axis=1)
        spread = jnp.broadcast_to(line, (lanes, lanes))
        limits.append(spread if transposed else spread.T)
    reach = (row if transposed else col).astype(f32)
    distance = jnp.abs(row - col).astype(f32)
    inside = same & (reach >= limits[0]) & (reach <= limits[1])
    return jnp.where(inside, jnp.exp(-distance / vertical_scale), 0.0)


def static_blocks(static_ref, levels):
    variables = static_ref.shape[0]
    lanes = variables * levels
    same = lane_grid(lanes, levels)[2]
    tiles = [jnp.concatenate([static_ref[v]] * variables, axis=1) for v in range(variables)]
    return jnp.where(same, jnp.concatenate(tiles, axis=0), 0.0)


def pack_row(dims, ring, first_rows, last_rows, y, value):
    rows, levels, width, variables, depth = dims
    ring[depth + y, pl.ds(2 * SIDE, width)] = value
    if y < depth:
        first_rows[y] = value.astype(bf16)
    if y >= rows - depth:
        last_rows[y - (rows - depth)] = value.astype(bf16)


def band_selector(owner, groups):
    def band_of(group):
        result = 0
        for b in range(groups):
            result = result + jnp.where(owner[0, b] == group, b, 0)
        return result

    return band_of


def choose(index, options):
    result = options[0]
    for place in range(1, len(options)):
        result = jnp.where(index == place, options[place], result)
    return result


def coded(value):
    largest = jnp.maximum(jnp.max(jnp.abs(value), axis=0, keepdims=True), 1e-30)
    codes = jnp.round(value * (code_limit / largest)).astype(jnp.int16)
    return codes, jnp.broadcast_to(largest * (1.0 / code_limit), (SIDE, value.shape[1]))


def step_kernel(
    dims, ens_scale, owner, count, bounds, static_vert, kappa, jacobian_ref, anchor_hbm, weight_hbm,
    background_hbm, observed_hbm, inv_var_hbm, alpha_hbm, chi_hbm, perturb_hbm, out_alpha, out_chi,
    alpha, chi, perturb, anchor_ref, weight_ref, background_ref, observed_ref, inv_var_ref, kap,
    ring, back_ring, work, rows_out, rows_in, back_rows_out, back_rows_in, kappa_in, field, nat,
    static, mix, partial, high, low, table, base, rim_out, rim_in, near_out, near_in, far_out,
    far_in, near_code, near_scale, far_code, far_scale, near_codes, near_scales, far_codes,
    far_scales, turn_out, turn_scale, turn_in, turn_scale_in, grad, load, send, recv, ring_send,
    ring_recv,
):
    rows, levels, width, variables, depth = dims
    groups, lanes = ring.shape[0], ring.shape[3]
    cell_count, column = rows * levels, variables * levels
    group_rows, group_members = lanes * rows, lanes // levels
    members = perturb.shape[0]
    inner = pl.ds(2 * SIDE, width)
    split_count = lax.axis_size("mem")
    me, gx, gx_count = lax.axis_index("mem"), lax.axis_index("gx"), lax.axis_size("gx")
    east, west = {"gx": lax.rem(gx + 1, gx_count)}, {"gx": lax.rem(gx + gx_count - 1, gx_count)}
    hops = range(1, split_count)
    partners = [{"mem": lax.rem(me + hop, split_count)} for hop in hops]
    band = width // split_count
    shift = band // 2
    block = rows * shift
    places = anchor_ref.shape[1]

    greet_around(partners)
    group_part = [pl.ds(g * group_rows, group_rows) for g in range(groups)]
    loads = [
        pltpu.make_async_copy(alpha_hbm.at[part], alpha.at[part], load.at[g])
        for g, part in enumerate(group_part)
    ]
    others = [
        pltpu.make_async_copy(source, target, load.at[groups + i])
        for i, (source, target) in enumerate(
            [
                (chi_hbm, chi), (perturb_hbm, perturb), (anchor_hbm, anchor_ref),
                (weight_hbm, weight_ref), (background_hbm, background_ref),
                (observed_hbm, observed_ref), (inv_var_hbm, inv_var_ref),
            ]
        )
    ]
    for item in loads + others:
        item.start()

    def ring_moves(target, out_rows, in_rows, first):
        return [
            ring_copies(
                dims, target.at[g], out_rows.at[g, 0], out_rows.at[g, 1], in_rows.at[g, 0],
                in_rows.at[g, 1], ring_send.at[first + g], ring_recv.at[first + g],
            )
            for g in range(groups)
        ]

    moves = ring_moves(ring, rows_out, rows_in, 0)
    back_moves = ring_moves(back_ring, back_rows_out, back_rows_in, groups)
    move_kappa = ring_copies(
        dims, kap, kappa.at[pl.ds(0, SIDE)], kappa.at[pl.ds(rows - SIDE, SIDE)], kappa_in.at[0],
        kappa_in.at[1], ring_send.at[2 * groups], ring_recv.at[2 * groups],
    )

    def pack_group(g, source, target, out_rows):
        for y in range(rows):
            held = source[pl.ds(g * group_rows + y, lanes, stride=rows), :]
            pack_row(dims, target.at[g], out_rows.at[g, 0], out_rows.at[g, 1], y, held.T)

    for g in range(groups):
        loads[g].wait()
        pack_group(g, alpha, ring, rows_out)
        if g == 0:
            wait_around(len(partners))
        moves[g][0]()
        if g == 0:
            for y in range(rows):
                kap[depth + y, inner] = jnp.broadcast_to(kappa[y : y + 1, :], (lanes, width)).T
            move_kappa[0]()
    mix[...] = stacked_weights(
        static_blocks(static_vert, levels) * jnp.where(me == 0, static_weight, 0.0)
    )
    others[0].wait()
    for y in range(0, rows, 2):
        pair = [chi[pl.ds(y + i, column, stride=rows), :] for i in (0, 1)]
        both = mixed(mix, jnp.concatenate(pair, axis=1), 0)
        static[y], static[y + 1] = both[:, :width], both[:, width:]

    mix[...] = stacked_weights(vertical_blocks(bounds, lanes, levels, False))
    for item in others[2:]:
        item.wait()
    base[...] = background_ref[...].astype(f32).T

    @pl.loop(0, places // lanes)
    def _(chunk):
        here = pl.ds(pl.multiple_of(chunk * lanes, lanes), lanes)
        anchor = anchor_ref[:, here]
        anchor_row = anchor // band
        anchor_col = anchor - anchor_row * band
        weight = [weight_ref[q : q + 1, here] for q in range(4)]
        slot = lax.broadcasted_iota(jnp.int32, (band, lanes), 0)
        at_left, at_right = slot == anchor_col, slot == anchor_col + 1
        parts = [
            split(
                jnp.where(
                    at_left, weight[2 * d], jnp.where(at_right, weight[2 * d + 1], 0.0)
                )
            )
            for d in range(2)
        ]
        spread_row = jnp.broadcast_to(anchor_row, (shift, lanes))
        for y in range(rows):
            upper = jnp.where(spread_row == y, 1.0, 0.0).astype(bf16)
            lower = jnp.where(spread_row == y - 1, 1.0, 0.0).astype(bf16)
            for half in range(2):
                cut = slice(half * shift, (half + 1) * shift)
                place = pl.ds(half * block + y * shift, shift)
                for ref, term in ((high, 0), (low, 1)):
                    ref[place, here] = parts[0][term][cut] * upper + parts[1][term][cut] * lower
        line = lax.broadcasted_iota(jnp.int32, (rows, lanes), 0)
        past = anchor_col == band - 1
        ends = jnp.where(
            past & (line == anchor_row), weight[1],
            jnp.where(past & (line == anchor_row + 1), weight[3], 0.0),
        )
        final = pl.ds(2 * block, rows)
        high[final, here], low[final, here] = split(ends)

    move_kappa[1]()
    fill_halo_rows(
        dims, kap,
        lambda d: jnp.broadcast_to(kappa_in[0, d : d + 1, :], (lanes, width)).T,
        lambda d: jnp.broadcast_to(
            kappa_in[1, SIDE - depth + d : SIDE - depth + d + 1, :], (lanes, width)
        ).T,
    )

    def diffused(g, source, in_rows, copies):
        copies[g][1]()
        fill_halo_rows(
            dims, source.at[g], lambda d: in_rows[g, 0, d].astype(f32),
            lambda d: in_rows[g, 1, d].astype(f32),
        )
        diffuse(dims, source.at[g], work, kap)
        for y in range(0, rows, 2):
            pair = [source[g, depth + y + i, inner] for i in (0, 1)]
            both = mixed(mix, jnp.concatenate(pair, axis=0), 1)
            for i in (0, 1):
                yield y + i, pl.ds(g * group_rows + y + i, lanes, stride=rows), both[
                    :, i * width : (i + 1) * width
                ]

    for g in range(groups):
        for y, line, value in diffused(g, ring, rows_in, moves):
            field[line, :] = value
    others[1].wait()

    @pl.loop(0, levels)
    def _(level):
        place = pl.multiple_of(level * rows, rows)
        spreads = [field[pl.ds(k * cell_count + place, rows), :] for k in range(members)]
        for v in range(variables):
            total = perturb[0, v, pl.ds(place, rows), :].astype(f32) * spreads[0]
            for k in range(1, members):
                total = total + perturb[k, v, pl.ds(place, rows), :].astype(f32) * spreads[k]
            nat[pl.ds(v * cell_count + place, rows), :] = total

    for y in range(rows):
        partial[y] = (ens_scale * nat[pl.ds(y, column, stride=rows), :] + static[y]).T

    def copy(source, target, kind, hop, device):
        return pltpu.make_async_remote_copy(
            src_ref=source, dst_ref=target, send_sem=send.at[kind, hop],
            recv_sem=recv.at[kind, hop], device_id=device, device_id_type=pl.DeviceIdType.MESH,
        )

    def to_partners(source, target, kind, each):
        return [
            copy(source.at[h - 1] if each else source, target.at[h - 1], kind, h, partners[h - 1])
            for h in hops
        ]

    move_rim = copy(rim_out, rim_in, 0, 0, west)
    move_near = to_partners(near_out, near_in, 1, True)
    move_far = to_partners(far_out, far_in, 2, True)
    move_turn = [
        copy(turn_out, turn_in, 1, 0, east), copy(turn_scale, turn_scale_in, 2, 0, east)
    ]
    back_far = to_partners(far_code, far_codes, 3, False)
    back_far += to_partners(far_scale, far_scales, 4, False)
    back_near = to_partners(near_code, near_codes, 5, False)
    back_near += to_partners(near_scale, near_scales, 6, False)

    band_of = band_selector(owner, split_count)
    away = [band_of(lax.rem(me + hop, split_count)) for hop in hops]
    own_band = band_of(me)

    def columns(start):
        return jnp.concatenate([partial[y, pl.ds(start, shift), :] for y in range(rows)], axis=0)

    def edge(start):
        return jnp.concatenate([partial[y, pl.ds(start, 1), :] for y in range(rows)], axis=0)

    def near_of(index):
        return choose(index, [columns(b * band + shift) for b in range(split_count)])

    def far_of(index):
        options = [
            jnp.concatenate([columns(b * band), edge(b * band + shift)], axis=0)
            for b in range(1, split_count)
        ]
        return choose(index, options + [rim_in[...].astype(f32)])

    rim_out[...] = jnp.concatenate([columns(0), edge(shift)], axis=0).astype(bf16)
    move_rim.start()
    for h in hops:
        near_out[h - 1] = near_of(away[h - 1]).astype(bf16)
        move_near[h - 1].start()
    move_rim.wait_recv()
    for h in hops:
        far_out[h - 1] = far_of(away[h - 1]).astype(bf16)
        move_far[h - 1].start()
    near, far = near_of(own_band), far_of(own_band)
    for h in hops:
        move_near[h - 1].wait_recv()
        near = near + near_in[h - 1].astype(f32)
    table[pl.ds(0, block), :] = near.astype(bf16)
    for h in hops:
        move_far[h - 1].wait_recv()
        far = far + far_in[h - 1].astype(f32)
    table[pl.ds(block, block + rows), :] = far.astype(bf16)

    cells = table[...]
    total = base[...] + lax.dot_general(cells, high[...], TN, preferred_element_type=f32)
    total = total + lax.dot_general(cells, low[...], TN, preferred_element_type=f32)
    bent = jnp.tanh(total)
    jacobian = jacobian_ref[...]
    channels = jacobian.shape[0]
    modeled = lax.dot_general(
        stacked_weights(jacobian), jnp.concatenate(split(bent), axis=0), NN,
        preferred_element_type=f32,
    )
    modeled = modeled[:channels] + modeled[channels:]
    position = lax.broadcasted_iota(jnp.int32, modeled.shape, 1)
    misfit = jnp.where(
        position < count[0], (modeled - observed_ref[...]) * inv_var_ref[...], 0.0
    )
    misfit_high = misfit.astype(bf16).astype(f32)
    jacobian_high = jacobian.astype(bf16).astype(f32)
    back = lax.dot_general(
        jnp.concatenate(
            [jacobian_high, jacobian_high, jacobian - jacobian_high, jnp.zeros_like(jacobian)],
            axis=0,
        ).astype(bf16),
        jnp.concatenate(
            [misfit_high, misfit - misfit_high, misfit_high, jnp.zeros_like(misfit)], axis=0
        ).astype(bf16),
        TN, preferred_element_type=f32,
    )
    state_high, state_low = split((1.0 - bent * bent) * back)
    states = jnp.concatenate([state_high, state_low], axis=0)

    def cells_of(start, size):
        here = pl.ds(start, size)
        both = lax.dot_general(high[here, :], states, NT, preferred_element_type=f32)
        rest = lax.dot_general(low[here, :], state_high, NT, preferred_element_type=f32)
        return both[:, :column] + both[:, column:] + rest

    far_code[...], far_scale[...] = coded(cells_of(block, block + rows))
    for item in back_far:
        item.start()
    near_code[...], near_scale[...] = coded(cells_of(0, block))
    for item in back_near:
        item.start()

    def hop_of(index):
        gap = me - owner[0, index]
        return jnp.where(gap < 0, gap + split_count, gap)

    def fars(index, scales):
        own, rest = (far_scale, far_scales) if scales else (far_code, far_codes)
        values = [own[...]] + [rest[h - 1] for h in hops]
        return choose(hop_of(index), values if scales else [v.astype(jnp.int32) for v in values])

    for item in back_far:
        item.wait_recv()
    turn_out[...] = fars(split_count - 1, False).astype(jnp.int16)
    turn_scale[...] = fars(split_count - 1, True)
    for item in move_turn:
        item.start()
    mix[...] = stacked_weights(static_weight * static_blocks(static_vert, levels).T)
    ends = []
    for b in range(split_count - 1):
        value = fars(b, False).astype(f32) * fars(b, True)[:1]
        for y in range(rows):
            grad[y, pl.ds((b + 1) * band, shift), :] = value[y * shift : (y + 1) * shift]
        ends.append(value[block:])
    for item in back_near:
        item.wait_recv()
    nears = [near_code[...]] + [near_codes[h - 1] for h in hops]
    nears = [v.astype(jnp.int32) for v in nears]
    near_steps = [near_scale[...]] + [near_scales[h - 1] for h in hops]
    for b in range(split_count):
        value = choose(hop_of(b), nears).astype(f32) * choose(hop_of(b), near_steps)[:1]
        for y in range(rows):
            grad[y, pl.ds(b * band + shift, shift), :] = value[y * shift : (y + 1) * shift]
    for item in move_turn:
        item.wait_recv()
    turned = turn_in[...].astype(f32) * turn_scale_in[:1]
    for y in range(rows):
        grad[y, pl.ds(0, shift), :] = turned[y * shift : (y + 1) * shift]
    for b, value in enumerate([turned[block:]] + ends):
        place = pl.ds(b * band + shift, 1)
        for y in range(rows):
            grad[y, place, :] = grad[y, place, :] + value[y : y + 1]

    for y in range(rows):
        nat[pl.ds(y, column, stride=rows), :] = ens_scale * grad[y].T
    for g in range(groups):

        @pl.loop(0, levels)
        def _(level, g=g):
            place = pl.multiple_of(level * rows, rows)
            slopes = [nat[pl.ds(v * cell_count + place, rows), :] for v in range(variables)]
            for k in range(g * group_members, (g + 1) * group_members):
                total = perturb[k, 0, pl.ds(place, rows), :].astype(f32) * slopes[0]
                for v in range(1, variables):
                    total = total + perturb[k, v, pl.ds(place, rows), :].astype(f32) * slopes[v]
                field[pl.ds(k * cell_count + place, rows), :] = total * kappa[...]

        pack_group(g, field, back_ring, back_rows_out)
        back_moves[g][0]()
    for y in range(0, rows, 2):
        both = mixed(mix, jnp.concatenate([grad[y], grad[y + 1]], axis=0), 1)
        for i in (0, 1):
            line = pl.ds(y + i, column, stride=rows)
            out_chi[line, :] = chi[line, :] + both[:, i * width : (i + 1) * width]
    mix[...] = stacked_weights(vertical_blocks(bounds, lanes, levels, True))
    inverse = 1.0 / kappa[...]
    for g in range(groups):
        for y, line, value in diffused(g, back_ring, back_rows_in, back_moves):
            out_alpha[line, :] = alpha[line, :] + inverse[y : y + 1] * value
    for item in [move_rim] + move_turn + move_near + move_far + back_near + back_far:
        item.wait_send()


def body(
    alpha, perturb, chi, kappa, vert_bounds, static_vert, fine_owner, obs_stencil, obs_weight,
    background, observed, inv_var, jacobian, obs_count,
):
    members, levels, rows, width = alpha.shape
    variables = perturb.shape[1]
    column = variables * levels
    depth = NDIFF
    count = rows * levels
    dims = (rows, levels, width, variables, depth)
    ens_scale = ensemble_weight / math.sqrt(members * lax.axis_size("mem") - 1)
    split_count = lax.axis_size("mem")
    places = obs_stencil.shape[0]
    shift = width // split_count // 2
    block = rows * shift
    grouped = members * levels // column
    ring_shape = (rows + 2 * depth, width + 4 * SIDE, column)
    smem = pl.BlockSpec(memory_space=pltpu.SMEM)
    vmem = pl.BlockSpec(memory_space=pltpu.VMEM)
    hbm = pl.BlockSpec(memory_space=pltpu.HBM)
    rings = pltpu.VMEM((grouped,) + ring_shape, f32)
    row_pairs = pltpu.VMEM((grouped, 2, depth, width, column), bf16)
    alpha_tile = pltpu.VMEM((members * count, width), f32)
    chi_tile = pltpu.VMEM((variables * count, width), f32)
    near, far = (block, column), (block + rows, column)
    scale = (SIDE, column)
    away = (split_count - 1,)
    i16 = jnp.int16
    grad_alpha, grad_chi = pl.pallas_call(
        lambda *refs: step_kernel(dims, ens_scale, *refs),
        in_specs=[smem, smem] + [vmem] * 4 + [hbm] * 8,
        out_specs=[vmem, vmem],
        out_shape=[
            jax.ShapeDtypeStruct((members * count, width), f32),
            jax.ShapeDtypeStruct((variables * count, width), f32),
        ],
        scratch_shapes=[
            alpha_tile,
            chi_tile,
            pltpu.VMEM((members, variables, count, width), bf16),
            pltpu.VMEM((1, places), jnp.int32),
            pltpu.VMEM((4, places), f32),
            pltpu.VMEM((places, column), bf16),
            pltpu.VMEM(observed.shape, f32),
            pltpu.VMEM(inv_var.shape, f32),
            pltpu.VMEM(ring_shape, f32),
            rings,
            rings,
            pltpu.VMEM(ring_shape, f32),
            row_pairs,
            row_pairs,
            row_pairs,
            row_pairs,
            pltpu.VMEM((2, SIDE, width), f32),
            alpha_tile,
            chi_tile,
            pltpu.VMEM((rows, column, width), f32),
            pltpu.VMEM((2 * column, 2 * column), bf16),
            pltpu.VMEM((rows, width, column), f32),
            pltpu.VMEM((2 * block + rows, places), bf16),
            pltpu.VMEM((2 * block + rows, places), bf16),
            pltpu.VMEM((2 * block + rows, column), bf16),
            pltpu.VMEM((column, places), f32),
            pltpu.VMEM(far, bf16),
            pltpu.VMEM(far, bf16),
            pltpu.VMEM(away + near, bf16),
            pltpu.VMEM(away + near, bf16),
            pltpu.VMEM(away + far, bf16),
            pltpu.VMEM(away + far, bf16),
            pltpu.VMEM(near, i16),
            pltpu.VMEM(scale, f32),
            pltpu.VMEM(far, i16),
            pltpu.VMEM(scale, f32),
            pltpu.VMEM(away + near, i16),
            pltpu.VMEM(away + scale, f32),
            pltpu.VMEM(away + far, i16),
            pltpu.VMEM(away + scale, f32),
            pltpu.VMEM(far, i16),
            pltpu.VMEM(scale, f32),
            pltpu.VMEM(far, i16),
            pltpu.VMEM(scale, f32),
            pltpu.VMEM((rows, width, column), f32),
            pltpu.SemaphoreType.DMA((grouped + 7,)),
            pltpu.SemaphoreType.DMA((7, split_count)),
            pltpu.SemaphoreType.DMA((7, split_count)),
            pltpu.SemaphoreType.DMA((2 * grouped + 1, 8)),
            pltpu.SemaphoreType.DMA((2 * grouped + 1, 8)),
        ],
        compiler_params=pltpu.CompilerParams(
            collective_id=0, has_side_effects=True, vmem_limit_bytes=60 << 20
        ),
        name="step",
    )(
        fine_owner, obs_count, vert_bounds, static_vert, kappa, jacobian,
        obs_stencil.reshape(1, places), obs_weight, background, observed, inv_var,
        alpha.reshape(members * count, width), chi.reshape(variables * count, width),
        perturb.reshape(members, variables, count, width),
    )
    return grad_alpha.reshape(alpha.shape), grad_chi.reshape(chi.shape)


def solution(mesh):
    in_specs = (
        P("mem", None, "gy", "gx"),
        P("mem", None, None, "gy", "gx"),
        P(None, None, "gy", "gx"),
        P("gy", "gx"),
        P(),
        P(),
        P(("gy", "gx"), None),
        P(("mem", "gy", "gx")),
        P(None, ("mem", "gy", "gx")),
        P(("mem", "gy", "gx"), None),
        P(None, ("mem", "gy", "gx")),
        P(None, ("mem", "gy", "gx")),
        P(),
        P(("mem", "gy", "gx")),
    )
    out_specs = (P("mem", None, "gy", "gx"), P(None, None, "gy", "gx"))
    return jax.shard_map(body, mesh=mesh, in_specs=in_specs, out_specs=out_specs, check_vma=False)
```

time: 87.7 us -> 57.9 us (0.66)
  waiting for transfers between devices: 16.7 us -> 0 us
  local copies, waits for them, and re-layouts: 14.3 us -> 4.11 us
  Pallas kernels: 42.4 us -> 51.7 us
  starting transfers between devices: 6.46 us -> 0 us
  other arithmetic: 2.88 us -> 0 us
  between operations: 4.05 us -> 1.3 us
    ppermute x6 -> x0, waiting for transfers between devices: 16.7 us -> none  [shifted(): return lax.ppermute(value, axis, pairs)]
    pallas_call x3 -> x1, Pallas kernels: 42.4 us -> 51.7 us  [body(): pl.pallas_call(lambda *refs: step_kernel(dims, ens_scale, *refs), in_spec...]
    unnamed x32 -> x4, local copies, waits for them, and re-layouts: 12.3 us -> 4.11 us
    ppermute x6 -> x0, starting transfers between devices: 6.46 us -> none  [shifted(): return lax.ppermute(value, axis, pairs)]
    slice x3 -> x0, local copies, waits for them, and re-layouts: 2 us -> none  [the longest x1 1 us: body(): region_grad[:, band - shift:band + 1]]
    select_n x2 -> x0, other arithmetic: 1.16 us -> none  [choose_equal(): result = jnp.where(index == wanted, piece, result)]
  transfers between devices with their start and end apart: 6 -> 0, of which waited for: 5 -> 0; matrix products, arithmetic and copies ran while one was open for 2% -> 0% of each run, Pallas kernels for 0% -> 0%
where the time goes in v1:
time: 57.9 us; the launch traced here: 57.1 us
  Pallas kernels  51.7 us (89%)
  local copies, waits for them, and re-layouts  4.11 us (7%)
  between operations  1.3 us (2%)
    pallas_call x1, Pallas kernels, body(): pl.pallas_call(lambda *refs: step_kernel(dims, ens_scale, *refs), in_spec...  51.7 us
    unnamed x4, local copies, waits for them, and re-layouts  4.11 us

profile of v1, /device:TPU:0, one launch (start us, length us, event | category | flops | bytes accessed | tf_op | source)
XLA Modules:
  0.0 57.1 jit_solution(12737988658139430317)
XLA Ops:
  1.3 51.7 %step.1 = (f32[4096,128]{1,0:T(8,128)}, f32[2048,128]{1,0:T(8,128)}) custom-call(s32[1,2]{1,0:T(1,128)} %refs_0_.1, s32[1]{0:T(128)S(6)} %copy.18.refs_1_, s32[2,32]{1,0:T(2,128)} %refs_2_.1, f32[4,32,32]{2,1,0:T(8,128)} %refs_3_.1, f32[16,128]{1,0:T(8,128)} %refs_4_.1, f32[8,128]{1,0:T(8,128)} %refs_5_.1, s32[1,1024]{1,0:T(1,128)} %bitcast.11, ...), custom_call_target="tpu_custom_call" | custom-call | tf_op jit(solution)/shard_map/step/pallas_call | solution.py:629
  53.0 0.0 copy-start
  53.0 3.1 %copy.19 = f32[8,32,16,128]{3,2,1,0:T(8,128)} copy(f32[8,32,16,128]{3,2,1,0:T(8,128)} %bitcast.7) | data formatting | bytes 4194304
  56.1 0.0 copy-done
  56.1 1.0 %copy.20 = f32[4,32,16,128]{3,2,1,0:T(8,128)} copy(f32[4,32,16,128]{3,2,1,0:T(8,128)S(1)} %bitcast.10) | data formatting | bytes 2097152
Async XLA Ops:
  53.0 3.1 %copy-start = (f32[2048,128]{1,0:T(8,128)S(1)}, f32[2048,128]{1,0:T(8,128)}, u32[]{:S(2)}) copy-start(f32[2048,128]{1,0:T(8,128)} %get-tuple-element.5) | copy-start | bytes 3145732

commit v2 on v1

--- a/solution.py
+++ b/solution.py
@@ -255,10 +255,25 @@
     return codes, jnp.broadcast_to(largest * (1.0 / code_limit), (SIDE, value.shape[1]))
 
 
+def unpack_kernel(alpha_rows, chi_rows, out_alpha, out_chi, done):
+    rows = alpha_rows.shape[0]
+    moves = []
+    for i, (source, target) in enumerate([(alpha_rows, out_alpha), (chi_rows, out_chi)]):
+        moves += [
+            pltpu.make_async_copy(source.at[y], target.at[:, y, :], done.at[i, y])
+            for y in range(rows)
+        ]
+    for item in moves:
+        item.start()
+    for item in moves:
+        item.wait()
+
+
 def step_kernel(
-    dims, ens_scale, owner, count, bounds, static_vert, kappa, jacobian_ref, anchor_hbm, weight_hbm,
-    background_hbm, observed_hbm, inv_var_hbm, alpha_hbm, chi_hbm, perturb_hbm, out_alpha, out_chi,
-    alpha, chi, perturb, anchor_ref, weight_ref, background_ref, observed_ref, inv_var_ref, kap,
+    dims, ens_scale, owner, count, alpha_hbm, chi_hbm, perturb_hbm, kappa_hbm, static_hbm,
+    bounds_hbm, jacobian_hbm, anchor_hbm, weight_hbm, background_hbm, observed_hbm, inv_var_hbm,
+    out_alpha, out_chi, alpha, chi, perturb, kappa, static_vert, bounds, jacobian_ref, anchor_ref,
+    weight_ref, background_ref, observed_ref, inv_var_ref, kap,
     ring, back_ring, work, rows_out, rows_in, back_rows_out, back_rows_in, kappa_in, field, nat,
     static, mix, partial, high, low, table, base, rim_out, rim_in, near_out, near_in, far_out,
     far_in, near_code, near_scale, far_code, far_scale, near_codes, near_scales, far_codes,
@@ -267,8 +282,9 @@
 ):
     rows, levels, width, variables, depth = dims
     groups, lanes = ring.shape[0], ring.shape[3]
-    cell_count, column = rows * levels, variables * levels
-    group_rows, group_members = lanes * rows, lanes // levels
+    column = variables * levels
+    group_members = lanes // levels
+    pitch = rows + SIDE // 2
     members = perturb.shape[0]
     inner = pl.ds(2 * SIDE, width)
     split_count = lax.axis_size("mem")
@@ -282,23 +298,37 @@
     places = anchor_ref.shape[1]
 
     greet_around(partners)
-    group_part = [pl.ds(g * group_rows, group_rows) for g in range(groups)]
-    loads = [
-        pltpu.make_async_copy(alpha_hbm.at[part], alpha.at[part], load.at[g])
-        for g, part in enumerate(group_part)
+    load_alpha = [
+        [
+            pltpu.make_async_copy(
+                alpha_hbm.at[pl.ds(g * lanes, lanes), y, :],
+                alpha.at[y, pl.ds(g * lanes, lanes), :], load.at[g * rows + y],
+            )
+            for y in range(rows)
+        ]
+        for g in range(groups)
+    ]
+    used = groups * rows
+    load_chi = [
+        pltpu.make_async_copy(chi_hbm.at[:, y, :], chi.at[y], load.at[used + y])
+        for y in range(rows)
+    ]
+    used += rows
+    pairs = [
+        (kappa_hbm, kappa), (static_hbm, static_vert), (bounds_hbm, bounds),
+        (jacobian_hbm, jacobian_ref), (anchor_hbm, anchor_ref), (weight_hbm, weight_ref),
+        (background_hbm, background_ref), (observed_hbm, observed_ref), (inv_var_hbm, inv_var_ref),
+        (perturb_hbm, perturb),
     ]
     others = [
-        pltpu.make_async_copy(source, target, load.at[groups + i])
-        for i, (source, target) in enumerate(
-            [
-                (chi_hbm, chi), (perturb_hbm, perturb), (anchor_hbm, anchor_ref),
-                (weight_hbm, weight_ref), (background_hbm, background_ref),
-                (observed_hbm, observed_ref), (inv_var_hbm, inv_var_ref),
-            ]
-        )
+        pltpu.make_async_copy(source, target, load.at[used + i])
+        for i, (source, target) in enumerate(pairs)
     ]
-    for item in loads + others:
+    for item in load_alpha[0] + others[:1]:
         item.start()
+    for part in load_alpha[1:] + [load_chi, others[1:]]:
+        for item in part:
+            item.start()
 
     def ring_moves(target, out_rows, in_rows, first):
         return [
@@ -316,33 +346,38 @@
         kappa_in.at[1], ring_send.at[2 * groups], ring_recv.at[2 * groups],
     )
 
-    def pack_group(g, source, target, out_rows):
+    def pack_group(g, held_row, target, out_rows):
         for y in range(rows):
-            held = source[pl.ds(g * group_rows + y, lanes, stride=rows), :]
-            pack_row(dims, target.at[g], out_rows.at[g, 0], out_rows.at[g, 1], y, held.T)
+            pack_row(
+                dims, target.at[g], out_rows.at[g, 0], out_rows.at[g, 1], y, held_row(y).T
+            )
 
     for g in range(groups):
-        loads[g].wait()
-        pack_group(g, alpha, ring, rows_out)
+        for item in load_alpha[g]:
+            item.wait()
+        pack_group(g, lambda y: alpha[y, pl.ds(g * lanes, lanes), :], ring, rows_out)
         if g == 0:
             wait_around(len(partners))
         moves[g][0]()
         if g == 0:
+            others[0].wait()
             for y in range(rows):
                 kap[depth + y, inner] = jnp.broadcast_to(kappa[y : y + 1, :], (lanes, width)).T
             move_kappa[0]()
+    others[1].wait()
     mix[...] = stacked_weights(
         static_blocks(static_vert, levels) * jnp.where(me == 0, static_weight, 0.0)
     )
-    others[0].wait()
+    for item in load_chi:
+        item.wait()
     for y in range(0, rows, 2):
-        pair = [chi[pl.ds(y + i, column, stride=rows), :] for i in (0, 1)]
+        pair = [chi[y + i] for i in (0, 1)]
         both = mixed(mix, jnp.concatenate(pair, axis=1), 0)
         static[y], static[y + 1] = both[:, :width], both[:, width:]
 
+    for item in others[2:-1]:
+        item.wait()
     mix[...] = stacked_weights(vertical_blocks(bounds, lanes, levels, False))
-    for item in others[2:]:
-        item.wait()
     base[...] = background_ref[...].astype(f32).T
 
     @pl.loop(0, places // lanes)
@@ -400,27 +435,28 @@
             pair = [source[g, depth + y + i, inner] for i in (0, 1)]
             both = mixed(mix, jnp.concatenate(pair, axis=0), 1)
             for i in (0, 1):
-                yield y + i, pl.ds(g * group_rows + y + i, lanes, stride=rows), both[
-                    :, i * width : (i + 1) * width
-                ]
+                yield y + i, both[:, i * width : (i + 1) * width]
 
     for g in range(groups):
-        for y, line, value in diffused(g, ring, rows_in, moves):
-            field[line, :] = value
-    others[1].wait()
+        for y, value in diffused(g, ring, rows_in, moves):
+            field[pl.ds(g * lanes * pitch + y, lanes, stride=pitch), :] = value
+    others[-1].wait()
+
+    def field_rows(k, level):
+        return pl.ds(pl.multiple_of((k * levels + level) * pitch, SIDE // 2), rows)
 
     @pl.loop(0, levels)
     def _(level):
         place = pl.multiple_of(level * rows, rows)
-        spreads = [field[pl.ds(k * cell_count + place, rows), :] for k in range(members)]
+        spreads = [field[field_rows(k, level), :] for k in range(members)]
         for v in range(variables):
             total = perturb[0, v, pl.ds(place, rows), :].astype(f32) * spreads[0]
             for k in range(1, members):
                 total = total + perturb[k, v, pl.ds(place, rows), :].astype(f32) * spreads[k]
-            nat[pl.ds(v * cell_count + place, rows), :] = total
+            nat[field_rows(v, level), :] = total
 
     for y in range(rows):
-        partial[y] = (ens_scale * nat[pl.ds(y, column, stride=rows), :] + static[y]).T
+        partial[y] = (ens_scale * nat[pl.ds(y, column, stride=pitch), :] + static[y]).T
 
     def copy(source, target, kind, hop, device):
         return pltpu.make_async_remote_copy(
@@ -569,31 +605,34 @@
             grad[y, place, :] = grad[y, place, :] + value[y : y + 1]
 
     for y in range(rows):
-        nat[pl.ds(y, column, stride=rows), :] = ens_scale * grad[y].T
+        nat[pl.ds(y, column, stride=pitch), :] = ens_scale * grad[y].T
     for g in range(groups):
 
         @pl.loop(0, levels)
         def _(level, g=g):
             place = pl.multiple_of(level * rows, rows)
-            slopes = [nat[pl.ds(v * cell_count + place, rows), :] for v in range(variables)]
+            slopes = [nat[field_rows(v, level), :] for v in range(variables)]
             for k in range(g * group_members, (g + 1) * group_members):
                 total = perturb[k, 0, pl.ds(place, rows), :].astype(f32) * slopes[0]
                 for v in range(1, variables):
                     total = total + perturb[k, v, pl.ds(place, rows), :].astype(f32) * slopes[v]
-                field[pl.ds(k * cell_count + place, rows), :] = total * kappa[...]
-
-        pack_group(g, field, back_ring, back_rows_out)
+                field[field_rows(k, level), :] = total * kappa[...]
+
+        pack_group(
+            g, lambda y: field[pl.ds(g * lanes * pitch + y, lanes, stride=pitch), :], back_ring,
+            back_rows_out,
+        )
         back_moves[g][0]()
     for y in range(0, rows, 2):
         both = mixed(mix, jnp.concatenate([grad[y], grad[y + 1]], axis=0), 1)
         for i in (0, 1):
-            line = pl.ds(y + i, column, stride=rows)
-            out_chi[line, :] = chi[line, :] + both[:, i * width : (i + 1) * width]
+            out_chi[y + i] = chi[y + i] + both[:, i * width : (i + 1) * width]
     mix[...] = stacked_weights(vertical_blocks(bounds, lanes, levels, True))
     inverse = 1.0 / kappa[...]
     for g in range(groups):
-        for y, line, value in diffused(g, back_ring, back_rows_in, back_moves):
-            out_alpha[line, :] = alpha[line, :] + inverse[y : y + 1] * value
+        here = pl.ds(g * lanes, lanes)
+        for y, value in diffused(g, back_ring, back_rows_in, back_moves):
+            out_alpha[y, here, :] = alpha[y, here, :] + inverse[y : y + 1] * value
     for item in [move_rim] + move_turn + move_near + move_far + back_near + back_far:
         item.wait_send()
 
@@ -620,24 +659,27 @@
     hbm = pl.BlockSpec(memory_space=pltpu.HBM)
     rings = pltpu.VMEM((grouped,) + ring_shape, f32)
     row_pairs = pltpu.VMEM((grouped, 2, depth, width, column), bf16)
-    alpha_tile = pltpu.VMEM((members * count, width), f32)
-    chi_tile = pltpu.VMEM((variables * count, width), f32)
+    pitch = rows + SIDE // 2
+    alpha_shape, chi_shape = (rows, members * levels, width), (rows, column, width)
     near, far = (block, column), (block + rows, column)
     scale = (SIDE, column)
     away = (split_count - 1,)
     i16 = jnp.int16
     grad_alpha, grad_chi = pl.pallas_call(
         lambda *refs: step_kernel(dims, ens_scale, *refs),
-        in_specs=[smem, smem] + [vmem] * 4 + [hbm] * 8,
+        in_specs=[smem, smem] + [hbm] * 12,
         out_specs=[vmem, vmem],
         out_shape=[
-            jax.ShapeDtypeStruct((members * count, width), f32),
-            jax.ShapeDtypeStruct((variables * count, width), f32),
+            jax.ShapeDtypeStruct(alpha_shape, f32), jax.ShapeDtypeStruct(chi_shape, f32)
         ],
         scratch_shapes=[
-            alpha_tile,
-            chi_tile,
+            pltpu.VMEM(alpha_shape, f32),
+            pltpu.VMEM(chi_shape, f32),
             pltpu.VMEM((members, variables, count, width), bf16),
+            pltpu.VMEM(kappa.shape, f32),
+            pltpu.VMEM(static_vert.shape, f32),
+            pltpu.VMEM(vert_bounds.shape, jnp.int32),
+            pltpu.VMEM(jacobian.shape, f32),
             pltpu.VMEM((1, places), jnp.int32),
             pltpu.VMEM((4, places), f32),
             pltpu.VMEM((places, column), bf16),
@@ -652,8 +694,8 @@
             row_pairs,
             row_pairs,
             pltpu.VMEM((2, SIDE, width), f32),
-            alpha_tile,
-            chi_tile,
+            pltpu.VMEM((members * levels * pitch, width), f32),
+            pltpu.VMEM((column * pitch, width), f32),
             pltpu.VMEM((rows, column, width), f32),
             pltpu.VMEM((2 * column, 2 * column), bf16),
             pltpu.VMEM((rows, width, column), f32),
@@ -680,22 +722,37 @@
             pltpu.VMEM(far, i16),
             pltpu.VMEM(scale, f32),
             pltpu.VMEM((rows, width, column), f32),
-            pltpu.SemaphoreType.DMA((grouped + 7,)),
+            pltpu.SemaphoreType.DMA(((grouped + 1) * rows + 10,)),
             pltpu.SemaphoreType.DMA((7, split_count)),
             pltpu.SemaphoreType.DMA((7, split_count)),
             pltpu.SemaphoreType.DMA((2 * grouped + 1, 8)),
             pltpu.SemaphoreType.DMA((2 * grouped + 1, 8)),
         ],
         compiler_params=pltpu.CompilerParams(
-            collective_id=0, has_side_effects=True, vmem_limit_bytes=60 << 20
+            collective_id=0, has_side_effects=True, vmem_limit_bytes=44 << 20
         ),
         name="step",
     )(
-        fine_owner, obs_count, vert_bounds, static_vert, kappa, jacobian,
-        obs_stencil.reshape(1, places), obs_weight, background, observed, inv_var,
-        alpha.reshape(members * count, width), chi.reshape(variables * count, width),
-        perturb.reshape(members, variables, count, width),
-    )
+        fine_owner, obs_count,
+        *[
+            pltpu.with_memory_space_constraint(value, pltpu.HBM)
+            for value in (
+                alpha.reshape(members * levels, rows, width), chi.reshape(column, rows, width),
+                perturb.reshape(members, variables, count, width), kappa, static_vert, vert_bounds,
+                jacobian, obs_stencil.reshape(1, places), obs_weight, background, observed, inv_var,
+            )
+        ],
+    )
+    alpha_out, chi_out = (members * levels, rows, width), (column, rows, width)
+    grad_alpha, grad_chi = pl.pallas_call(
+        unpack_kernel,
+        in_specs=[vmem, vmem],
+        out_specs=[hbm, hbm],
+        out_shape=[jax.ShapeDtypeStruct(alpha_out, f32), jax.ShapeDtypeStruct(chi_out, f32)],
+        scratch_shapes=[pltpu.SemaphoreType.DMA((2, rows))],
+        compiler_params=pltpu.CompilerParams(vmem_limit_bytes=16 << 20),
+        name="unpack",
+    )(grad_alpha, grad_chi)
     return grad_alpha.reshape(alpha.shape), grad_chi.reshape(chi.shape)
 
 

time: 57.9 us -> 54.1 us (0.934)
  local copies, waits for them, and re-layouts: 4.11 us -> 0.65 us
    unnamed x4 -> x2, local copies, waits for them, and re-layouts: 4.11 us -> 0.65 us
    pallas_call x1, Pallas kernels: 51.7 us -> 49.4 us  [body(): pl.pallas_call(lambda *refs: step_kernel(dims, ens_scale, *refs), in_spec...]
    pallas_call x0 -> x1, Pallas kernels: none -> 1.92 us  [body(): pl.pallas_call(unpack_kernel, in_specs=[vmem, vmem], out_specs=[hbm, hbm]...]
where the time goes in v2:
time: 54.1 us; the launch traced here: 53.3 us
  Pallas kernels  51.3 us (95%)
  between operations  1.3 us (2%)
  local copies, waits for them, and re-layouts  0.65 us (1%)
    pallas_call x1, Pallas kernels, body(): pl.pallas_call(lambda *refs: step_kernel(dims, ens_scale, *refs), in_spec...  49.4 us
    pallas_call x1, Pallas kernels, body(): pl.pallas_call(unpack_kernel, in_specs=[vmem, vmem], out_specs=[hbm, hbm]...  1.92 us

profile of v2, /device:TPU:0, one launch (start us, length us, event | category | flops | bytes accessed | tf_op | source)
XLA Modules:
  0.0 53.3 jit_solution(7913971465850766472)
XLA Ops:
  1.3 0.0 copy-start
  1.3 0.6 %copy-done = s32[1,2]{1,0:T(1,128)S(1)} copy-done((s32[1,2]{1,0:T(1,128)S(1)}, s32[1,2]{1,0:T(1,128)}, u32[]{:S(2)}) %copy-start) | copy-done | bytes 32
  1.9 49.4 %step.1 = (f32[16,256,128]{2,1,0:T(8,128)S(1)}, f32[16,128,128]{2,1,0:T(8,128)S(1)}) custom-call(s32[1,2]{1,0:T(1,128)S(1)} %copy-done, s32[1]{0:T(128)S(6)} %copy.16.refs_1_, f32[256,16,128]{2,1,0:T(8,128)} %bitcast.7, f32[128,16,128]{2,1,0:T(8,128)} %bitcast.8, bf16[8,4,512,128]{3,2,1,0:T(8,128)(2,1)} %bitcast.6, f32[16,128]{1,0:T(8,128)} %refs_5_.1, ...), custom_call_target="tpu_custom_call" | custom-call | tf_op jit(solution)/shard_map/step/pallas_call | solution.py:668
  51.4 1.9 %unpack.1 = (f32[256,16,128]{2,1,0:T(8,128)}, f32[128,16,128]{2,1,0:T(8,128)}) custom-call(f32[16,256,128]{2,1,0:T(8,128)S(1)} %get-tuple-element.6.alpha_rows, f32[16,128,128]{2,1,0:T(8,128)S(1)} %get-tuple-element.7.chi_rows), custom_call_target="tpu_custom_call" | custom-call | tf_op jit(solution)/shard_map/unpack/pallas_call | solution.py:747
Async XLA Ops:
  1.3 0.7 %copy-start = (s32[1,2]{1,0:T(1,128)S(1)}, s32[1,2]{1,0:T(1,128)}, u32[]{:S(2)}) copy-start(s32[1,2]{1,0:T(1,128)} %refs_0_.1) | copy-start | bytes 28

commit v3 on v2

--- a/solution.py
+++ b/solution.py
@@ -57,13 +57,13 @@
     pl.semaphore_wait(pltpu.get_barrier_semaphore(), peers)
 
 
-def ring_copies(dims, ring, first_rows, last_rows, south_in, north_in, send, recv):
+def ring_copies(dims, ring, corners, first_rows, last_rows, south_in, north_in, send, recv):
     rows, levels, width, variables, depth = dims
     east, west, north, south, has_north, has_south = compass()
-    top, bottom = pl.ds(depth, depth), pl.ds(rows, depth)
     body, above, below = pl.ds(depth, rows), pl.ds(0, depth), pl.ds(depth + rows, depth)
-    first, last = pl.ds(2 * SIDE, SIDE), pl.ds(SIDE + width, SIDE)
-    before, after = pl.ds(SIDE, SIDE), pl.ds(2 * SIDE + width, SIDE)
+    first, last = pl.ds(2 * SIDE, depth), pl.ds(2 * SIDE + width - depth, depth)
+    before, after = pl.ds(2 * SIDE - depth, depth), pl.ds(2 * SIDE + width, depth)
+    left, right = pl.ds(0, depth), pl.ds(SIDE - depth, depth)
 
     def copy(source, target, place, device):
         return pltpu.make_async_remote_copy(
@@ -77,16 +77,19 @@
     ]
     up = [
         copy(first_rows, south_in, 2, {"gy": north}),
-        copy(ring.at[top, last], ring.at[below, before], 3, {"gy": north, "gx": east}),
-        copy(ring.at[top, first], ring.at[below, after], 4, {"gy": north, "gx": west}),
+        copy(corners.at[0, :, right], ring.at[below, before], 3, {"gy": north, "gx": east}),
+        copy(corners.at[1, :, left], ring.at[below, after], 4, {"gy": north, "gx": west}),
     ]
     down = [
         copy(last_rows, north_in, 5, {"gy": south}),
-        copy(ring.at[bottom, last], ring.at[above, before], 6, {"gy": south, "gx": east}),
-        copy(ring.at[bottom, first], ring.at[above, after], 7, {"gy": south, "gx": west}),
+        copy(corners.at[2, :, right], ring.at[above, before], 6, {"gy": south, "gx": east}),
+        copy(corners.at[3, :, left], ring.at[above, after], 7, {"gy": south, "gx": west}),
     ]
 
     def start():
+        for item in across:
+            item.start()
+
         @pl.when(has_north)
         def _():
             for item in up:
@@ -97,14 +100,12 @@
             for item in down:
                 item.start()
 
-        for item in across:
-            item.start()
-
-    def wait():
+    def wait_across():
         for item in across:
             item.wait_recv()
             item.wait_send()
 
+    def wait_rows():
         @pl.when(has_north)
         def _():
             for item in down:
@@ -119,44 +120,66 @@
             for item in down:
                 item.wait_send()
 
-    return start, wait
+    return start, wait_across, wait_rows
+
+
+def save_corners(dims, ring, corners):
+    rows, levels, width, variables, depth = dims
+    for i, y in enumerate((depth, depth, rows, rows)):
+        x = 2 * SIDE if i % 2 else SIDE + width
+        corners[i] = ring[pl.ds(y, depth), pl.ds(x, SIDE)]
+
+
+def mirror_rows(dims, ring):
+    rows, levels, width, variables, depth = dims
+    east, west, north, south, has_north, has_south = compass()
+    whole = pl.ds(SIDE, width + 2 * SIDE)
+
+    @pl.when(jnp.logical_not(has_south))
+    def _():
+        for d in range(depth):
+            ring[depth + rows + d, whole] = ring[depth + rows - 1 - d, whole]
+
+    @pl.when(jnp.logical_not(has_north))
+    def _():
+        for d in range(depth):
+            ring[d, whole] = ring[2 * depth - 1 - d, whole]
 
 
 def fill_halo_rows(dims, ring, from_south, from_north):
     rows, levels, width, variables, depth = dims
     east, west, north, south, has_north, has_south = compass()
-    inner, whole = pl.ds(2 * SIDE, width), pl.ds(SIDE, width + 2 * SIDE)
+    inner = pl.ds(2 * SIDE, width)
 
     @pl.when(has_south)
     def _():
         for d in range(depth):
             ring[depth + rows + d, inner] = from_south(d)
 
-    @pl.when(jnp.logical_not(has_south))
-    def _():
-        for d in range(depth):
-            ring[depth + rows + d, whole] = ring[depth + rows - 1 - d, whole]
-
     @pl.when(has_north)
     def _():
         for d in range(depth):
             ring[d, inner] = from_north(d)
 
-    @pl.when(jnp.logical_not(has_north))
-    def _():
-        for d in range(depth):
-            ring[d, whole] = ring[2 * depth - 1 - d, whole]
-
-
-def diffuse(dims, ring, work, kap):
+
+def diffuse(dims, ring, work, kap, inside):
     rows, levels, width, variables, depth = dims
     for step in range(1, depth + 1):
         source, target = (ring, work) if step % 2 else (work, ring)
         start, stop = (SIDE, width + 3 * SIDE) if step < depth else (2 * SIDE, width + 2 * SIDE)
-
-        @pl.loop(0, rows // 2 + depth - step)
-        def _(pair, source=source, target=target, start=start, stop=stop, step=step):
-            y = step + 2 * pair
+        if inside:
+            count, first, skip = rows // 2 - step, depth + step, 0
+        else:
+            count, first, skip = depth, step, rows - 2 * step
+
+        @pl.loop(0, count)
+        def _(
+            pair, source=source, target=target, start=start, stop=stop, first=first, skip=skip,
+            count=count,
+        ):
+            y = first + 2 * pair
+            if skip:
+                y = y + jnp.where(pair >= count // 2, skip, 0)
             for x in range(start, stop, 6 * SIDE):
                 size = min(6 * SIDE, stop - x)
                 here = pl.ds(x, size)
@@ -274,7 +297,7 @@
     bounds_hbm, jacobian_hbm, anchor_hbm, weight_hbm, background_hbm, observed_hbm, inv_var_hbm,
     out_alpha, out_chi, alpha, chi, perturb, kappa, static_vert, bounds, jacobian_ref, anchor_ref,
     weight_ref, background_ref, observed_ref, inv_var_ref, kap,
-    ring, back_ring, work, rows_out, rows_in, back_rows_out, back_rows_in, kappa_in, field, nat,
+    ring, back_ring, work, corners, rows_out, rows_in, back_rows_out, back_rows_in, kappa_in, field, nat,
     static, mix, partial, high, low, table, base, rim_out, rim_in, near_out, near_in, far_out,
     far_in, near_code, near_scale, far_code, far_scale, near_codes, near_scales, far_codes,
     far_scales, turn_out, turn_scale, turn_in, turn_scale_in, grad, load, send, recv, ring_send,
@@ -333,8 +356,8 @@
     def ring_moves(target, out_rows, in_rows, first):
         return [
             ring_copies(
-                dims, target.at[g], out_rows.at[g, 0], out_rows.at[g, 1], in_rows.at[g, 0],
-                in_rows.at[g, 1], ring_send.at[first + g], ring_recv.at[first + g],
+                dims, target.at[g], corners.at[first + g], out_rows.at[g, 0], out_rows.at[g, 1],
+                in_rows.at[g, 0], in_rows.at[g, 1], ring_send.at[first + g], ring_recv.at[first + g],
             )
             for g in range(groups)
         ]
@@ -342,20 +365,21 @@
     moves = ring_moves(ring, rows_out, rows_in, 0)
     back_moves = ring_moves(back_ring, back_rows_out, back_rows_in, groups)
     move_kappa = ring_copies(
-        dims, kap, kappa.at[pl.ds(0, SIDE)], kappa.at[pl.ds(rows - SIDE, SIDE)], kappa_in.at[0],
-        kappa_in.at[1], ring_send.at[2 * groups], ring_recv.at[2 * groups],
-    )
-
-    def pack_group(g, held_row, target, out_rows):
+        dims, kap, corners.at[2 * groups], kappa.at[pl.ds(0, SIDE)],
+        kappa.at[pl.ds(rows - SIDE, SIDE)], kappa_in.at[0], kappa_in.at[1], ring_send.at[2 * groups], ring_recv.at[2 * groups],
+    )
+
+    def pack_group(g, held_row, target, out_rows, place):
         for y in range(rows):
             pack_row(
                 dims, target.at[g], out_rows.at[g, 0], out_rows.at[g, 1], y, held_row(y).T
             )
+        save_corners(dims, target.at[g], corners.at[place + g])
 
     for g in range(groups):
         for item in load_alpha[g]:
             item.wait()
-        pack_group(g, lambda y: alpha[y, pl.ds(g * lanes, lanes), :], ring, rows_out)
+        pack_group(g, lambda y: alpha[y, pl.ds(g * lanes, lanes), :], ring, rows_out, 0)
         if g == 0:
             wait_around(len(partners))
         moves[g][0]()
@@ -363,6 +387,7 @@
             others[0].wait()
             for y in range(rows):
                 kap[depth + y, inner] = jnp.broadcast_to(kappa[y : y + 1, :], (lanes, width)).T
+            save_corners(dims, kap, corners.at[2 * groups])
             move_kappa[0]()
     others[1].wait()
     mix[...] = stacked_weights(
@@ -416,6 +441,16 @@
         high[final, here], low[final, here] = split(ends)
 
     move_kappa[1]()
+    mirror_rows(dims, kap)
+
+    def diffuse_inside(source, copies):
+        for g in range(groups):
+            copies[g][1]()
+            mirror_rows(dims, source.at[g])
+            diffuse(dims, source.at[g], work.at[g], kap, True)
+
+    diffuse_inside(ring, moves)
+    move_kappa[2]()
     fill_halo_rows(
         dims, kap,
         lambda d: jnp.broadcast_to(kappa_in[0, d : d + 1, :], (lanes, width)).T,
@@ -425,12 +460,12 @@
     )
 
     def diffused(g, source, in_rows, copies):
-        copies[g][1]()
+        copies[g][2]()
         fill_halo_rows(
             dims, source.at[g], lambda d: in_rows[g, 0, d].astype(f32),
             lambda d: in_rows[g, 1, d].astype(f32),
         )
-        diffuse(dims, source.at[g], work, kap)
+        diffuse(dims, source.at[g], work.at[g], kap, False)
         for y in range(0, rows, 2):
             pair = [source[g, depth + y + i, inner] for i in (0, 1)]
             both = mixed(mix, jnp.concatenate(pair, axis=0), 1)
@@ -620,7 +655,7 @@
 
         pack_group(
             g, lambda y: field[pl.ds(g * lanes * pitch + y, lanes, stride=pitch), :], back_ring,
-            back_rows_out,
+            back_rows_out, groups,
         )
         back_moves[g][0]()
     for y in range(0, rows, 2):
@@ -629,6 +664,7 @@
             out_chi[y + i] = chi[y + i] + both[:, i * width : (i + 1) * width]
     mix[...] = stacked_weights(vertical_blocks(bounds, lanes, levels, True))
     inverse = 1.0 / kappa[...]
+    diffuse_inside(back_ring, back_moves)
     for g in range(groups):
         here = pl.ds(g * lanes, lanes)
         for y, value in diffused(g, back_ring, back_rows_in, back_moves):
@@ -688,7 +724,8 @@
             pltpu.VMEM(ring_shape, f32),
             rings,
             rings,
-            pltpu.VMEM(ring_shape, f32),
+            rings,
+            pltpu.VMEM((2 * grouped + 1, 4, depth, SIDE, column), f32),
             row_pairs,
             row_pairs,
             row_pairs,
@@ -729,7 +766,7 @@
             pltpu.SemaphoreType.DMA((2 * grouped + 1, 8)),
         ],
         compiler_params=pltpu.CompilerParams(
-            collective_id=0, has_side_effects=True, vmem_limit_bytes=44 << 20
+            collective_id=0, has_side_effects=True, vmem_limit_bytes=48 << 20
         ),
         name="step",
     )(

time: 54.1 us -> 50.8 us (0.939)
  Pallas kernels: 51.3 us -> 48.3 us
    pallas_call x1, Pallas kernels: 49.4 us -> 46.4 us  [body(): pl.pallas_call(lambda *refs: step_kernel(dims, ens_scale, *refs), in_spec...]
where the time goes in v3:
time: 50.8 us; the launch traced here: 50.2 us
  Pallas kernels  48.3 us (95%)
  between operations  1.3 us (3%)
  local copies, waits for them, and re-layouts  0.65 us (1%)
    pallas_call x1, Pallas kernels, body(): pl.pallas_call(lambda *refs: step_kernel(dims, ens_scale, *refs), in_spec...  46.4 us
    pallas_call x1, Pallas kernels, body(): pl.pallas_call(unpack_kernel, in_specs=[vmem, vmem], out_specs=[hbm, hbm]...  1.92 us

profile of v3, /device:TPU:0, one launch (start us, length us, event | category | flops | bytes accessed | tf_op | source)
XLA Modules:
  0.0 50.2 jit_solution(4205554450033360156)
XLA Ops:
  1.3 0.0 copy-start
  1.3 0.6 %copy-done = s32[1,2]{1,0:T(1,128)S(1)} copy-done((s32[1,2]{1,0:T(1,128)S(1)}, s32[1,2]{1,0:T(1,128)}, u32[]{:S(2)}) %copy-start) | copy-done | bytes 32
  1.9 46.4 %step.1 = (f32[16,256,128]{2,1,0:T(8,128)S(1)}, f32[16,128,128]{2,1,0:T(8,128)S(1)}) custom-call(s32[1,2]{1,0:T(1,128)S(1)} %copy-done, s32[1]{0:T(128)S(6)} %copy.16.refs_1_, f32[256,16,128]{2,1,0:T(8,128)} %bitcast.7, f32[128,16,128]{2,1,0:T(8,128)} %bitcast.8, bf16[8,4,512,128]{3,2,1,0:T(8,128)(2,1)} %bitcast.6, f32[16,128]{1,0:T(8,128)} %refs_5_.1, ...), custom_call_target="tpu_custom_call" | custom-call | tf_op jit(solution)/shard_map/step/pallas_call | solution.py:704
  48.3 1.9 %unpack.1 = (f32[256,16,128]{2,1,0:T(8,128)}, f32[128,16,128]{2,1,0:T(8,128)}) custom-call(f32[16,256,128]{2,1,0:T(8,128)S(1)} %get-tuple-element.6.alpha_rows, f32[16,128,128]{2,1,0:T(8,128)S(1)} %get-tuple-element.7.chi_rows), custom_call_target="tpu_custom_call" | custom-call | tf_op jit(solution)/shard_map/unpack/pallas_call | solution.py:784
Async XLA Ops:
  1.3 0.7 %copy-start = (s32[1,2]{1,0:T(1,128)S(1)}, s32[1,2]{1,0:T(1,128)}, u32[]{:S(2)}) copy-start(s32[1,2]{1,0:T(1,128)} %refs_0_.1) | copy-start | bytes 28
